TPU v7x, 128 devices: a whole 4x4x4 slice. The times are simulated.
128 devices in a mesh: dp: 16 (over x, y), expert: 8 (over z, core).
Axes of the slice: x: 4, y: 4, z: 4, core: 2. Of those that a mesh axis runs over, the one named last changes fastest.
Arguments:
- layer_input: bfloat16 [16384, 2560], P(('dp', 'expert')), may hold values from -6 to 6
- output_grad: bfloat16 [16384, 2560], P(('dp', 'expert')), may hold values from -6 to 6
- expert_ids: int32 [16384, 2], P(('dp', 'expert')), may hold values from 0 to 7, all different within a row; in each aligned block of 128 rows (0 to 127, 128 to 255, ...) at most 48 rows name the same one
- gate_probs: bfloat16 [16384, 2], P(('dp', 'expert')), may hold values from 0.099609375 to 0.59765625
- gate_weight: float32 [8, 2560, 1536], P('expert', 'dp'), may hold values from -0.125 to 0.125
- up_weight: float32 [8, 2560, 1536], P('expert', 'dp'), may hold values from -0.125 to 0.125
- down_weight: float32 [8, 1536, 2560], P('expert', 'dp'), may hold values from -0.15625 to 0.15625
- gate_moment: float32 [8, 2560, 1536], P('expert', 'dp'), may hold values from -12 to 12
- up_moment: float32 [8, 2560, 1536], P('expert', 'dp'), may hold values from -12 to 12
- down_moment: float32 [8, 1536, 2560], P('expert', 'dp'), may hold values from -12 to 12
- gate_second: float32 [8, 2560, 1536], P('expert', 'dp'), may hold values from 1 to 100
- up_second: float32 [8, 2560, 1536], P('expert', 'dp'), may hold values from 1 to 100
- down_second: float32 [8, 1536, 2560], P('expert', 'dp'), may hold values from 1 to 100
Outputs:
- input_grad: bfloat16 [16384, 2560], P(('dp', 'expert'))
- prob_grad: bfloat16 [16384, 2], P(('dp', 'expert'))
- new_gate_weight: float32 [8, 2560, 1536], P('expert', 'dp')
- new_up_weight: float32 [8, 2560, 1536], P('expert', 'dp')
- new_down_weight: float32 [8, 1536, 2560], P('expert', 'dp')
- new_gate_moment: float32 [8, 2560, 1536], P('expert', 'dp')
- new_up_moment: float32 [8, 2560, 1536], P('expert', 'dp')
- new_down_moment: float32 [8, 1536, 2560], P('expert', 'dp')
- new_gate_second: float32 [8, 2560, 1536], P('expert', 'dp')
- new_up_second: float32 [8, 2560, 1536], P('expert', 'dp')
- new_down_second: float32 [8, 1536, 2560], P('expert', 'dp')
Inputs may be any that keep to these rules, and one draw needn't show every extreme that they name: `expert_ids`: each token names 2 different experts. Among the (token, pick) pairs of one device's 128 tokens, no expert is named more than 48 times, and in every draw some device's tokens name some expert exactly 48 times.
All inputs are finite; a program needn't handle non-finite values.
Results may differ from a plain program's by a relative error of at most 0.025.
Values may be sent and summed in bfloat16 or wider, within the bound.
No kernel may reach another device: no remote copies, remote signals or barrier semaphores. Data moves between devices by JAX's collectives and lax.ppermute only.
A program may use at most 256 MiB of HBM per device.

v0:
```python
import jax
import jax.numpy as jnp
from jax import lax
from jax.sharding import PartitionSpec as P

beta_one = 0.9
beta_two = 0.95
learn_rate = 0.003
decay_rate = 0.1
epsilon = 1e-08
correct_one = 1.0 - 2.6561398887587e-05
correct_two = 1.0 - 0.005920529220333


def slot_tables(flat_ids, expert_count, exp_dev, groups, capacity):
    onehot = (flat_ids[:, None] == jnp.arange(expert_count, dtype=jnp.int32)[None, :]).astype(
        jnp.int32
    )
    before = jnp.cumsum(onehot, axis=0) - onehot
    ranked = jnp.sum(before * onehot, axis=1)
    device = flat_ids // exp_dev
    local = flat_ids % exp_dev
    return (local * groups + device) * capacity + ranked


def adamw(weight, moment, second, grad):
    moment_new = beta_one * moment + (1.0 - beta_one) * grad
    second_new = beta_two * second + (1.0 - beta_two) * grad * grad
    update = moment_new / correct_one / (jnp.sqrt(second_new / correct_two) + epsilon)
    return (weight - learn_rate * (update + decay_rate * weight), moment_new, second_new)


def body(
    layer_input,
    output_grad,
    expert_ids,
    gate_probs,
    gate_weight,
    up_weight,
    down_weight,
    gate_moment,
    up_moment,
    down_moment,
    gate_second,
    up_second,
    down_second,
):
    exp_dev = gate_weight.shape[0]
    hidden_units = gate_weight.shape[2]
    width = layer_input.shape[1]
    groups = lax.axis_size("expert")
    shards = lax.axis_size("dp")
    tok_count, picks = expert_ids.shape
    capacity = 3 * tok_count * picks // (2 * exp_dev * groups)
    slots = exp_dev * groups * capacity
    row_count = groups * capacity
    dest_slot = slot_tables(expert_ids.reshape(-1), exp_dev * groups, exp_dev, groups, capacity)
    owner = (
        jnp.zeros((slots,), jnp.int32)
        .at[dest_slot]
        .set(jnp.arange(tok_count * picks, dtype=jnp.int32) // picks)
    )
    filled = jnp.zeros((slots,), jnp.int32).at[dest_slot].set(1) > 0
    zero_val = jnp.zeros((), jnp.bfloat16)
    send_input = jnp.where(filled[:, None], layer_input[owner], zero_val).reshape(
        exp_dev, groups, capacity, width
    )
    send_grad = jnp.where(filled[:, None], output_grad[owner], zero_val).reshape(
        exp_dev, groups, capacity, width
    )
    send_gate = (
        jnp.zeros((slots,), jnp.bfloat16)
        .at[dest_slot]
        .set(gate_probs.reshape(-1))
        .reshape(exp_dev, groups, capacity)
    )
    w_gate_up_shard = jnp.concatenate((gate_weight, up_weight), axis=2).astype(jnp.bfloat16)
    w_down_shard = down_weight.astype(jnp.bfloat16)
    w_gate_up, w_down = (
        lax.all_gather(w_gate_up_shard, "dp", axis=1, tiled=True),
        lax.all_gather(w_down_shard, "dp", axis=1, tiled=True),
    )
    recv_input, recv_grad, recv_gate = (
        lax.all_to_all(send_input, "expert", split_axis=1, concat_axis=1, tiled=True),
        lax.all_to_all(send_grad, "expert", split_axis=1, concat_axis=1, tiled=True),
        lax.all_to_all(send_gate, "expert", split_axis=1, concat_axis=1, tiled=True),
    )
    x_rows = recv_input.reshape(exp_dev, row_count, width)
    dy_rows = recv_grad.reshape(exp_dev, row_count, width)
    gate_rows = recv_gate.reshape(exp_dev, row_count)
    pre = jnp.einsum("erd,edf->erf", x_rows, w_gate_up, preferred_element_type=jnp.float32)
    gate_pre = pre[:, :, :hidden_units]
    up_pre = pre[:, :, hidden_units:]
    sigmoid_gate = jax.nn.sigmoid(gate_pre)
    silu_gate = gate_pre * sigmoid_gate
    hidden = (silu_gate * up_pre).astype(jnp.bfloat16)
    expert_out = jnp.einsum("erf,efd->erd", hidden, w_down, preferred_element_type=jnp.float32)
    prob_rows = jnp.sum(dy_rows.astype(jnp.float32) * expert_out, axis=2).astype(jnp.bfloat16)
    out_scaled = (gate_rows.astype(jnp.float32)[:, :, None] * dy_rows.astype(jnp.float32)).astype(
        jnp.bfloat16
    )
    down_cols = hidden_units // shards
    model_cols = width // shards
    hidden_grad = jnp.einsum("erd,efd->erf", out_scaled, w_down, preferred_element_type=jnp.float32)
    dsilu = sigmoid_gate * (1.0 + gate_pre * (1.0 - sigmoid_gate))
    pre_grad = jnp.concatenate(
        (hidden_grad * up_pre * dsilu, hidden_grad * silu_gate), axis=2
    ).astype(jnp.bfloat16)
    input_rows = jnp.einsum(
        "erf,edf->erd", pre_grad, w_gate_up, preferred_element_type=jnp.float32
    ).astype(jnp.bfloat16)
    cols = x_rows
    first = jnp.einsum("erc,erf->cef", cols, pre_grad, preferred_element_type=jnp.float32).reshape(
        1 * lax.axis_size("dp"), model_cols * exp_dev * 2 * hidden_units
    )
    cols = hidden
    second = jnp.einsum(
        "erc,erd->ced", cols, out_scaled, preferred_element_type=jnp.float32
    ).reshape(1 * lax.axis_size("dp"), down_cols * exp_dev * width)
    joined = lax.psum_scatter(
        jnp.concatenate((first, second), axis=1).astype(jnp.bfloat16),
        "dp",
        scatter_dimension=0,
        tiled=True,
    ).astype(jnp.float32)
    split_at = model_cols * exp_dev * 2 * hidden_units
    grad_gate_up = joined[0, :split_at].reshape(model_cols, exp_dev, 2 * hidden_units)
    grad_down = joined[0, split_at:].reshape(down_cols, exp_dev, width)
    back_input, back_prob = (
        lax.all_to_all(
            input_rows.reshape(exp_dev, groups, capacity, width),
            "expert",
            split_axis=1,
            concat_axis=1,
            tiled=True,
        ),
        lax.all_to_all(
            prob_rows.reshape(exp_dev, groups, capacity),
            "expert",
            split_axis=1,
            concat_axis=1,
            tiled=True,
        ),
    )
    picked_rows = back_input.reshape(slots, width)[dest_slot].reshape(tok_count, picks, width)
    input_grad = jnp.sum(picked_rows.astype(jnp.float32), axis=1).astype(jnp.bfloat16)
    prob_grad = back_prob.reshape(slots)[dest_slot].reshape(tok_count, picks)
    grad_gate_up = jnp.transpose(grad_gate_up, (1, 0, 2))
    grad_down = jnp.transpose(grad_down, (1, 0, 2))
    new_gate_weight, new_gate_moment, new_gate_second = adamw(
        gate_weight, gate_moment, gate_second, grad_gate_up[:, :, :hidden_units]
    )
    new_up_weight, new_up_moment, new_up_second = adamw(
        up_weight, up_moment, up_second, grad_gate_up[:, :, hidden_units:]
    )
    new_down_weight, new_down_moment, new_down_second = adamw(
        down_weight, down_moment, down_second, grad_down
    )
    return (
        input_grad,
        prob_grad,
        new_gate_weight,
        new_up_weight,
        new_down_weight,
        new_gate_moment,
        new_up_moment,
        new_down_moment,
        new_gate_second,
        new_up_second,
        new_down_second,
    )


def solution(mesh):
    return jax.shard_map(
        body,
        mesh=mesh,
        in_specs=(
            P(("dp", "expert"), None),
            P(("dp", "expert"), None),
            P(("dp", "expert"), None),
            P(("dp", "expert"), None),
            P("expert", "dp", None),
            P("expert", "dp", None),
            P("expert", "dp", None),
            P("expert", "dp", None),
            P("expert", "dp", None),
            P("expert", "dp", None),
            P("expert", "dp", None),
            P("expert", "dp", None),
            P("expert", "dp", None),
        ),
        out_specs=(
            P(("dp", "expert"), None),
            P(("dp", "expert"), None),
            P("expert", "dp", None),
            P("expert", "dp", None),
            P("expert", "dp", None),
            P("expert", "dp", None),
            P("expert", "dp", None),
            P("expert", "dp", None),
            P("expert", "dp", None),
            P("expert", "dp", None),
            P("expert", "dp", None),
        ),
        check_vma=False,
    )
```

profile of v0, /device:TPU:1, one launch (start us, length us, event | category | flops | bytes accessed | tf_op | source)
XLA Modules:
  0.0 654.6 jit_solution(8457311708946021603)
XLA Ops:
  7.2 1.3 convert.31
  8.6 1.3 convert.30
  9.9 1.0 pad_maximum_fusion.4
  11.1 0.8 convert_element_type.131
  12.6 0.6 reduce-window.6
  13.8 2.2 scatter_custom_fusion
  16.0 0.7 reshape.417
  16.7 6.8 %all-to-all-start = ((bf16[1,8,48]{2,0,1:T(2,128)(2,1)}), bf16[1,8,48]{2,0,1:T(2,128)(2,1)S(1)}, u32[]{:S(2)}, u32[]{:S(2)}) async-start(bf16[1,8,48]{2,0,1:T(2,128)(2,1)} %reshape.417), calls=%async_computation | async-start | bytes 8192 | tf_op jit(solution)/shard_map/all_to_all | solution.py:86
  23.5 1.4 scatter_custom_fusion.2
  24.9 1.4 scatter_custom_fusion.1
  26.5 2.6 gather_fusion.1
  29.1 3.3 gather_fusion
  32.4 3.8 broadcast_select_fusion
  36.3 30.1 %all_to_all.25 = bf16[1,8,48,2560]{3,2,0,1:T(8,128)(2,1)S(1)} all-to-all(bf16[1,8,48,2560]{3,2,0,1:T(8,128)(2,1)} %get-tuple-element.60), channel_id=1, replica_groups=mesh['dp'=16,'expert'=8] {'expert'}, dimensions={1} | all-to-all | bytes 3932160 | tf_op jit(solution)/shard_map/all_to_all | solution.py:85
  66.3 5.1 all-to-all-start.2
  71.9 2.5 convert_element_type.140
  74.4 22.0 %all-to-all-done.2 = bf16[1,8,48,2560]{3,2,0,1:T(8,128)(2,1)} async-done(((bf16[1,8,48,2560]{3,2,0,1:T(8,128)(2,1)}), bf16[1,8,48,2560]{3,2,0,1:T(8,128)(2,1)}, u32[]{:S(2)}, u32[]{:S(2)}) %all-to-all-start.2) | async-done | bytes 1966112 | tf_op jit(solution)/shard_map/all_to_all | solution.py:84
  96.4 23.7 %all-gather.5.cloned.1.call-done = bf16[1,2560,3072]{2,1,0:T(8,128)(2,1)} async-done(((bf16[1,160,3072]{2,1,0:T(8,128)(2,1)}), bf16[1,2560,3072]{2,1,0:T(8,128)(2,1)}) %all-gather.5.cloned.1.call-update) | async-done | bytes 15728656 | tf_op jit(solution)/shard_map/all_gather | solution.py:80
  120.2 11.7 %fusion.13 = f32[1,384,3072]{2,1,0:T(8,128)} fusion(bf16[384,2560]{1,0:T(8,128)(2,1)} %bitcast.12, bf16[1,2560,3072]{2,1,0:T(8,128)(2,1)} %all-gather.5.cloned.1.call-done), kind=kOutput, calls=%fused_computation.21 | convolution fusion | flops 6039797760 | bytes 22413312 | tf_op jit(solution)/shard_map/erd,edf->erf/dot_general | solution.py:91
  131.8 59.3 %all-gather.3.cloned.1.call-done = bf16[1,1536,2560]{2,1,0:T(8,128)(2,1)} async-done(((bf16[1,96,2560]{2,1,0:T(8,128)(2,1)}), bf16[1,1536,2560]{2,1,0:T(8,128)(2,1)}) %all-gather.3.cloned.1.call-update) | async-done | bytes 7864336 | tf_op jit(solution)/shard_map/all_gather | solution.py:81
  191.1 10.8 %fusion.29 = (bf16[384,1536]{1,0:T(8,128)(2,1)S(1)}, bf16[384,1536]{1,0:T(8,128)(2,1)}, bf16[384,1536]{1,0:T(8,128)(2,1)S(1)}) fusion(f32[1,384,3072]{2,1,0:T(8,128)} %fusion.13, bf16[1,1536,2560]{2,1,0:T(8,128)(2,1)} %all-gather.3.cloned.1.call-done, f32[1,384,1,1,1,1,2560]{6,1,5,4,3,2,0:T(8,128)} %bitcast.83, f32[384]{0:T(512)S(1)} %reshape.356), kind=kOutput, calls=%fused_computation.42 | convolution fusion | flops 3030712320 | bytes 20055552 | tf_op jit(solution)/shard_map/erd,efd->erf/dot_general | solution.py:104
  201.9 6.6 %fusion.5 = bf16[1536,1,2560]{0,2,1:T(8,128)(2,1)} fusion(bf16[384,1536]{1,0:T(8,128)(2,1)S(1)} %get-tuple-element.55, f32[1,384,1,1,1,1,2560]{6,1,5,4,3,2,0:T(8,128)S(1)} %bitcast.85, f32[384]{0:T(512)S(1)} %reshape.356), kind=kOutput, calls=%fused_computation.15 | convolution fusion | flops 3025797120 | bytes 12977664 | tf_op jit(solution)/shard_map/erc,erd->ced/dot_general | solution.py:117
  208.5 10.6 %copy.51 = bf16[1536,1,2560]{2,0,1:T(8,128)(2,1)} copy(bf16[1536,1,2560]{0,2,1:T(8,128)(2,1)} %fusion.5) | data formatting | bytes 15728640 | tf_op jit(solution)/shard_map/erc,erd->ced/transpose | solution.py:117
  219.2 7.6 %reshape.355 = bf16[16,245760]{1,0:T(8,128)(2,1)} reshape(bf16[1536,1,2560]{2,0,1:T(8,128)(2,1)} %copy.51) | data formatting | bytes 15728640 | tf_op jit(solution)/shard_map/reshape | solution.py:119
  226.8 13.5 %fusion.4 = bf16[2560,1,3072]{0,2,1:T(8,128)(2,1)} fusion(bf16[384,2560]{1,0:T(8,128)(2,1)} %bitcast.12, bf16[384,1536]{1,0:T(8,128)(2,1)} %get-tuple-element.54, bf16[384,1536]{1,0:T(8,128)(2,1)S(1)} %get-tuple-element.53), kind=kOutput, calls=%fused_computation.13 | convolution fusion | flops 6052380672 | bytes 20054016 | tf_op jit(solution)/shard_map/erc,erf->cef/dot_general | solution.py:113
  240.3 20.7 %copy.50 = bf16[2560,1,3072]{2,0,1:T(8,128)(2,1)} copy(bf16[2560,1,3072]{0,2,1:T(8,128)(2,1)} %fusion.4) | data formatting | bytes 31457280 | tf_op jit(solution)/shard_map/erc,erf->cef/transpose | solution.py:113
  261.0 19.9 %reshape.354 = bf16[16,491520]{1,0:T(8,128)(2,1)} reshape(bf16[2560,1,3072]{2,0,1:T(8,128)(2,1)} %copy.50) | data formatting | bytes 31457280 | tf_op jit(solution)/shard_map/reshape | solution.py:113
  280.9 25.0 %pad_maximum_fusion = bf16[16,737280]{1,0:T(8,128)(2,1)} fusion(bf16[16,245760]{1,0:T(8,128)(2,1)} %reshape.355, bf16[16,491520]{1,0:T(8,128)(2,1)} %reshape.354), kind=kLoop, calls=%fused_computation.7 | loop fusion | flops 47185920 | bytes 47185920 | tf_op jit(solution)/shard_map/concatenate | solution.py:121
  305.9 7.6 %fusion.24 = bf16[384]{0:T(512)(128)(2,1)S(1)} fusion(f32[384,2560]{1,0:T(8,128)} %bitcast.84, bf16[384,1536]{1,0:T(8,128)(2,1)S(1)} %get-tuple-element.55, bf16[1,1536,2560]{2,1,0:T(8,128)(2,1)} %all-gather.3.cloned.1.call-done), kind=kOutput, calls=%fused_computation.36 | convolution fusion | flops 3021864448 | bytes 12976896 | tf_op jit(solution)/shard_map/erf,efd->erd/dot_general | solution.py:97
  313.6 0.7 convert_element_type.142
  314.3 5.1 all-to-all-start.4
  319.4 11.2 %fusion.16 = bf16[384,2560]{1,0:T(8,128)(2,1)} fusion(bf16[1,2560,3072]{2,1,0:T(8,128)(2,1)} %all-gather.5.cloned.1.call-done, bf16[384,1536]{1,0:T(8,128)(2,1)} %get-tuple-element.54, bf16[384,1536]{1,0:T(8,128)(2,1)S(1)} %get-tuple-element.53), kind=kOutput, calls=%fused_computation.22 | convolution fusion | flops 6045499392 | bytes 20054016 | tf_op jit(solution)/shard_map/erf,edf->erd/dot_general | solution.py:109
  330.6 5.2 all-to-all-start.3
  335.8 0.6 dynamic-slice
  336.5 1.9 gather_fusion.3
  338.6 0.6 copy.52
  339.2 21.5 %all-to-all-done.3 = bf16[1,8,48,2560]{3,2,0,1:T(8,128)(2,1)S(1)} async-done(((bf16[1,8,48,2560]{3,2,0,1:T(8,128)(2,1)}), bf16[1,8,48,2560]{3,2,0,1:T(8,128)(2,1)S(1)}, u32[]{:S(2)}, u32[]{:S(2)}) %all-to-all-start.3) | async-done | bytes 1966112 | tf_op jit(solution)/shard_map/all_to_all | solution.py:130
  360.6 2.6 gather_fusion.2
  363.2 3.1 reshape.350
  366.3 4.4 reduce_sum.34
  370.7 224.4 %all-reduce.3.cloned.1.call-done = bf16[16,737280]{1,0:T(8,128)(2,1)} async-done(((bf16[16,737280]{1,0:T(8,128)(2,1)}), bf16[16,737280]{1,0:T(8,128)(2,1)}) %all-reduce.3.cloned.1.call-update) | async-done | bytes 23592976
  595.0 7.3 %dynamic-slice_convert_fusion = f32[1,737280]{1,0:T(1,128)S(1)} fusion(bf16[16,737280]{1,0:T(8,128)(2,1)} %all-reduce.3.cloned.1.call-done, u32[]{:T(128)} %bitcast.32), kind=kLoop, calls=%fused_computation.25 | loop fusion | flops 737280 | bytes 4423684 | tf_op jit(solution)/shard_map/convert_element_type | solution.py:125
  602.4 21.6 %slice_reduce_fusion = f32[491520]{0:T(1024)} fusion(f32[1,737280]{1,0:T(1,128)S(1)} %dynamic-slice_convert_fusion), kind=kLoop, calls=%fused_computation.33 | loop fusion | bytes 3932160 | tf_op jit(solution)/shard_map/slice | solution.py:127
  624.0 11.3 %slice_reduce_fusion.1 = f32[245760]{0:T(1024)} fusion(f32[1,737280]{1,0:T(1,128)S(1)} %dynamic-slice_convert_fusion), kind=kLoop, calls=%fused_computation.46 | loop fusion | bytes 1966080 | tf_op jit(solution)/shard_map/slice | solution.py:128
  635.3 1.6 transpose_reshape_squeeze.6
  637.0 2.3 transpose_reshape_squeeze.7
  639.3 4.3 multiply_subtract_fusion
  643.9 3.7 multiply_subtract_fusion.1
  (62 shorter events, 2.7 us)
Async XLA Ops:
  7.2 19.3 %copy-start = (bf16[128,2560]{1,0:T(8,128)(2,1)S(1)}, bf16[128,2560]{1,0:T(8,128)(2,1)}, u32[]{:S(2)}) copy-start(bf16[128,2560]{1,0:T(8,128)(2,1)} %param.13) | copy-start | bytes 1966084
  7.2 113.0 %all-gather.5.cloned.1.call-start = ((), (), s32[]{:S(2)}) async-start(), calls=%async_computation.6 | async-start | bytes 16711680 | tf_op jit(solution)/shard_map/all_gather | solution.py:80
  8.6 2.5 copy-start.4
  9.9 2.0 copy-start.11
  9.9 3.5 copy-start.12
  11.0 180.1 %all-gather.3.cloned.1.call-start = ((), (), s32[]{:S(2)}) async-start(), calls=%async_computation.5 | async-start | bytes 8355840 | tf_op jit(solution)/shard_map/all_gather | solution.py:81
  16.7 19.6 %all-to-all-start = ((bf16[1,8,48]{2,0,1:T(2,128)(2,1)}), bf16[1,8,48]{2,0,1:T(2,128)(2,1)S(1)}, u32[]{:S(2)}, u32[]{:S(2)}) async-start(bf16[1,8,48]{2,0,1:T(2,128)(2,1)} %reshape.417), calls=%async_computation | async-start | bytes 8192 | tf_op jit(solution)/shard_map/all_to_all | solution.py:86
  26.5 2.6 copy-start.2
  66.3 30.1 %all-to-all-start.2 = ((bf16[1,8,48,2560]{3,2,0,1:T(8,128)(2,1)}), bf16[1,8,48,2560]{3,2,0,1:T(8,128)(2,1)}, u32[]{:S(2)}, u32[]{:S(2)}) async-start(bf16[1,8,48,2560]{3,2,0,1:T(8,128)(2,1)} %get-tuple-element.59), calls=%async_computation.2 | async-start | bytes 3932160 | tf_op jit(solution)/shard_map/all_to_all | solution.py:84
  71.4 523.7 %all-reduce.3.cloned.1.call-start = ((), (), s32[]{:S(2)}) async-start(), calls=%async_computation.7 | async-start | bytes 47185920
  191.1 10.8 %copy-start.3 = (f32[1,8,48,2560]{3,2,0,1:T(8,128)S(1)}, f32[1,8,48,2560]{3,2,0,1:T(8,128)}, u32[]{:S(2)}) copy-start(f32[1,8,48,2560]{3,2,0,1:T(8,128)} %convert_element_type.140) | copy-start | bytes 11796484
  314.3 16.3 %all-to-all-start.4 = ((bf16[1,8,48]{2,0,1:T(2,128)(2,1)}), bf16[1,8,48]{2,0,1:T(2,128)(2,1)S(1)}, u32[]{:S(2)}, u32[]{:S(2)}) async-start(bf16[1,8,48]{2,0,1:T(2,128)(2,1)} %convert_element_type.142), calls=%async_computation.4 | async-start | bytes 8192 | tf_op jit(solution)/shard_map/all_to_all | solution.py:137
  330.6 5.2 copy-start.13
  330.6 30.1 %all-to-all-start.3 = ((bf16[1,8,48,2560]{3,2,0,1:T(8,128)(2,1)}), bf16[1,8,48,2560]{3,2,0,1:T(8,128)(2,1)S(1)}, u32[]{:S(2)}, u32[]{:S(2)}) async-start(bf16[1,8,48,2560]{3,2,0,1:T(8,128)(2,1)} %bitcast.86), calls=%async_computation.3 | async-start | bytes 3932160 | tf_op jit(solution)/shard_map/all_to_all | solution.py:130
  639.2 4.4 copy-start.5
  639.2 4.4 copy-start.6
  639.3 4.4 copy-start.7
  639.3 4.4 copy-start.8
  639.3 4.4 copy-start.9
  639.3 4.7 copy-start.10
  643.9 3.7 copy-start.1
Sparse Core Ops, SparseCore 0:
  11.1 108.9 all-gather.4
  122.9 68.1 all-gather.2
  306.1 288.9 all-reduce.2
where the time goes:
time: 662 us; the launch traced here: 655 us
  waiting for transfers between devices  351 us (53%)
  local copies, waits for them, and re-layouts  119 us (18%)
  matrix products  61.4 us (9%)
  other arithmetic  56.3 us (9%)
  blocking collectives  30.1 us (5%)
  starting transfers between devices  22.7 us (3%)
  between operations  14.5 us (2%)
    unnamed x4, waiting for transfers between devices  224 us
    all_gather x1, waiting for transfers between devices, body(): lax.all_gather(w_down_shard, 'dp', axis=1, tiled=True)  59.3 us
    all_to_all x1, blocking collectives, body(): lax.all_to_all(send_grad, 'expert', split_axis=1, concat_axis=1, tiled=True)  30.1 us
    concatenate x1, other arithmetic, body(): jnp.concatenate((first, second), axis=1).astype(jnp.bfloat16)  25 us
    all_gather x1, waiting for transfers between devices, body(): lax.all_gather(w_gate_up_shard, 'dp', axis=1, tiled=True)  23.7 us
    all_to_all x1, waiting for transfers between devices, body(): lax.all_to_all(send_input, 'expert', split_axis=1, concat_axis=1, tiled=T...  22 us
    slice x1, local copies, waits for them, and re-layouts, body(): joined[0, :split_at].reshape(model_cols, exp_dev, 2 * hidden_units)  21.6 us
    all_to_all x1, waiting for transfers between devices, body(): lax.all_to_all(input_rows.reshape(exp_dev, groups, capacity, width), 'exp...  21.5 us
  transfers between devices with their start and end apart: 7, of which 5 were waited for; matrix products, arithmetic and copies ran while one was open for 10% of the time, Pallas kernels for 0%

commit v1 on v0

--- a/solution.py
+++ b/solution.py
@@ -49,7 +49,6 @@
     hidden_units = gate_weight.shape[2]
     width = layer_input.shape[1]
     groups = lax.axis_size("expert")
-    shards = lax.axis_size("dp")
     tok_count, picks = expert_ids.shape
     capacity = 3 * tok_count * picks // (2 * exp_dev * groups)
     slots = exp_dev * groups * capacity
@@ -93,15 +92,13 @@
     up_pre = pre[:, :, hidden_units:]
     sigmoid_gate = jax.nn.sigmoid(gate_pre)
     silu_gate = gate_pre * sigmoid_gate
-    hidden = (silu_gate * up_pre).astype(jnp.bfloat16)
-    expert_out = jnp.einsum("erf,efd->erd", hidden, w_down, preferred_element_type=jnp.float32)
-    prob_rows = jnp.sum(dy_rows.astype(jnp.float32) * expert_out, axis=2).astype(jnp.bfloat16)
-    out_scaled = (gate_rows.astype(jnp.float32)[:, :, None] * dy_rows.astype(jnp.float32)).astype(
-        jnp.bfloat16
-    )
-    down_cols = hidden_units // shards
-    model_cols = width // shards
-    hidden_grad = jnp.einsum("erd,efd->erf", out_scaled, w_down, preferred_element_type=jnp.float32)
+    hidden_full = silu_gate * up_pre
+    hidden = hidden_full.astype(jnp.bfloat16)
+    gate_col = gate_rows.astype(jnp.float32)[:, :, None]
+    raw_grad = jnp.einsum("erd,efd->erf", dy_rows, w_down, preferred_element_type=jnp.float32)
+    prob_rows = jnp.sum(hidden.astype(jnp.float32) * raw_grad, axis=2).astype(jnp.bfloat16)
+    hidden_scaled = (gate_col * hidden_full).astype(jnp.bfloat16)
+    hidden_grad = gate_col * raw_grad
     dsilu = sigmoid_gate * (1.0 + gate_pre * (1.0 - sigmoid_gate))
     pre_grad = jnp.concatenate(
         (hidden_grad * up_pre * dsilu, hidden_grad * silu_gate), axis=2
@@ -109,23 +106,18 @@
     input_rows = jnp.einsum(
         "erf,edf->erd", pre_grad, w_gate_up, preferred_element_type=jnp.float32
     ).astype(jnp.bfloat16)
-    cols = x_rows
-    first = jnp.einsum("erc,erf->cef", cols, pre_grad, preferred_element_type=jnp.float32).reshape(
-        1 * lax.axis_size("dp"), model_cols * exp_dev * 2 * hidden_units
+    second = jnp.einsum(
+        "erc,erd->ecd", hidden_scaled, dy_rows, preferred_element_type=jnp.float32
+    ).astype(jnp.bfloat16)
+    first = jnp.einsum(
+        "erc,erf->ecf", x_rows, pre_grad, preferred_element_type=jnp.float32
+    ).astype(jnp.bfloat16)
+    grad_down = lax.psum_scatter(second[0], "dp", scatter_dimension=0, tiled=True)[None].astype(
+        jnp.float32
     )
-    cols = hidden
-    second = jnp.einsum(
-        "erc,erd->ced", cols, out_scaled, preferred_element_type=jnp.float32
-    ).reshape(1 * lax.axis_size("dp"), down_cols * exp_dev * width)
-    joined = lax.psum_scatter(
-        jnp.concatenate((first, second), axis=1).astype(jnp.bfloat16),
-        "dp",
-        scatter_dimension=0,
-        tiled=True,
-    ).astype(jnp.float32)
-    split_at = model_cols * exp_dev * 2 * hidden_units
-    grad_gate_up = joined[0, :split_at].reshape(model_cols, exp_dev, 2 * hidden_units)
-    grad_down = joined[0, split_at:].reshape(down_cols, exp_dev, width)
+    grad_gate_up = lax.psum_scatter(first[0], "dp", scatter_dimension=0, tiled=True)[None].astype(
+        jnp.float32
+    )
     back_input, back_prob = (
         lax.all_to_all(
             input_rows.reshape(exp_dev, groups, capacity, width),
@@ -145,8 +137,6 @@
     picked_rows = back_input.reshape(slots, width)[dest_slot].reshape(tok_count, picks, width)
     input_grad = jnp.sum(picked_rows.astype(jnp.float32), axis=1).astype(jnp.bfloat16)
     prob_grad = back_prob.reshape(slots)[dest_slot].reshape(tok_count, picks)
-    grad_gate_up = jnp.transpose(grad_gate_up, (1, 0, 2))
-    grad_down = jnp.transpose(grad_down, (1, 0, 2))
     new_gate_weight, new_gate_moment, new_gate_second = adamw(
         gate_weight, gate_moment, gate_second, grad_gate_up[:, :, :hidden_units]
     )

time: 662 us -> 441 us (0.67)
  local copies, waits for them, and re-layouts: 119 us -> 24.1 us
  waiting for transfers between devices: 351 us -> 271 us
  other arithmetic: 56.3 us -> 24.3 us
  matrix products: 61.4 us -> 54.4 us
    unnamed x4, waiting for transfers between devices: 224 us -> 0.07 us
    reduce_scatter x0 -> x2, waiting for transfers between devices: none -> 131 us  [the longest x1 82.5 us: body(): lax.psum_scatter(second[0], 'dp', scatter_dimension=0, tiled=True)[None]]
    slice x3 -> x1, local copies, waits for them, and re-layouts: 33.1 us -> 0.21 us  [the longest x1 21.6 us: body(): joined[0, :split_at].reshape(model_cols, exp_dev, 2 * hidden_units)]
    transpose x2 -> x0, local copies, waits for them, and re-layouts: 31.3 us -> none  [the longest x1 20.7 us: body(): jnp.einsum('erc,erf->cef', cols, pre_grad, preferred_element_type=jnp.flo...]
    reshape x2 -> x0, local copies, waits for them, and re-layouts: 27.5 us -> none  [the longest x1 19.9 us: body(): jnp.einsum('erc,erf->cef', cols, pre_grad, preferred_element_type=jnp.flo...]
    all_gather x1, waiting for transfers between devices: 23.7 us -> 49 us  [body(): lax.all_gather(w_gate_up_shard, 'dp', axis=1, tiled=True)]
    concatenate x1 -> x0, other arithmetic: 25 us -> none  [body(): jnp.concatenate((first, second), axis=1).astype(jnp.bfloat16)]
    all_to_all x1, waiting for transfers between devices: 22 us -> 0.01 us  [body(): lax.all_to_all(send_grad, 'expert', split_axis=1, concat_axis=1, tiled=True)]
  transfers between devices with their start and end apart: 7 -> 8, of which waited for: 5 -> 5; matrix products, arithmetic and copies ran while one was open for 10% -> 12% of each run, Pallas kernels for 0% -> 0%
where the time goes in v1:
time: 441 us; the launch traced here: 440 us
  waiting for transfers between devices  271 us (61%)
  matrix products  54.4 us (12%)
  blocking collectives  29.9 us (7%)
  other arithmetic  24.3 us (6%)
  local copies, waits for them, and re-layouts  24.1 us (5%)
  starting transfers between devices  22.3 us (5%)
  between operations  14 us (3%)
    reduce_scatter x1, waiting for transfers between devices, body(): lax.psum_scatter(second[0], 'dp', scatter_dimension=0, tiled=True)[None]  82.5 us
    all_gather x1, waiting for transfers between devices, body(): lax.all_gather(w_down_shard, 'dp', axis=1, tiled=True)  68.9 us
    all_gather x1, waiting for transfers between devices, body(): lax.all_gather(w_gate_up_shard, 'dp', axis=1, tiled=True)  49 us
    reduce_scatter x1, waiting for transfers between devices, body(): lax.psum_scatter(first[0], 'dp', scatter_dimension=0, tiled=True)[None]  48.6 us
    all_to_all x1, blocking collectives, body(): lax.all_to_all(send_input, 'expert', split_axis=1, concat_axis=1, tiled=T...  29.9 us
    all_to_all x1, waiting for transfers between devices, body(): lax.all_to_all(input_rows.reshape(exp_dev, groups, capacity, width), 'exp...  22.1 us
    dot_general x1, matrix products, body(): jnp.einsum('erd,edf->erf', x_rows, w_gate_up, preferred_element_type=jnp....  12.2 us
    dot_general x1, matrix products, body(): jnp.einsum('erc,erf->ecf', x_rows, pre_grad, preferred_element_type=jnp.f...  11.5 us
  transfers between devices with their start and end apart: 8, of which 5 were waited for; matrix products, arithmetic and copies ran while one was open for 12% of the time, Pallas kernels for 0%

profile of v1, /device:TPU:1, one launch (start us, length us, event | category | flops | bytes accessed | tf_op | source)
XLA Modules:
  0.0 440.1 jit_solution(14314940471210939129)
XLA Ops:
  7.2 1.3 convert.18
  8.6 1.3 convert.17
  9.8 1.0 pad_maximum_fusion.3
  10.9 0.1 copy.38
  11.0 0.1 eq.31
  11.2 0.1 eq.27
  11.3 0.1 copy.37
  11.4 0.1 mul.150
  11.6 0.6 reduce-window.6
  12.2 0.2 slice_reduce_fusion
  12.4 0.1 copy.40
  12.6 0.2 reshape.293
  12.7 0.1 fusion.29
  12.8 2.2 scatter_custom_fusion
  15.0 0.7 reshape.315
  15.7 6.8 %all-to-all-start = ((bf16[1,8,48]{2,0,1:T(2,128)(2,1)}), bf16[1,8,48]{2,0,1:T(2,128)(2,1)S(1)}, u32[]{:S(2)}, u32[]{:S(2)}) async-start(bf16[1,8,48]{2,0,1:T(2,128)(2,1)} %reshape.315), calls=%async_computation | async-start | bytes 8192 | tf_op jit(solution)/shard_map/all_to_all | solution.py:85
  22.5 1.4 scatter_custom_fusion.2
  23.9 1.4 scatter_custom_fusion.1
  25.5 3.3 gather_fusion.1
  28.8 3.3 gather_fusion
  32.0 3.8 broadcast_select_fusion
  35.9 29.9 %all_to_all.25 = bf16[1,8,48,2560]{3,2,0,1:T(8,128)(2,1)} all-to-all(bf16[1,8,48,2560]{3,2,0,1:T(8,128)(2,1)S(1)} %get-tuple-element.60), channel_id=1, replica_groups=mesh['dp'=16,'expert'=8] {'expert'}, dimensions={1} | all-to-all | bytes 3932160 | tf_op jit(solution)/shard_map/all_to_all | solution.py:83
  65.8 5.2 %all-to-all-start.1 = ((bf16[1,8,48,2560]{3,2,0,1:T(8,128)(2,1)}), bf16[1,8,48,2560]{3,2,0,1:T(8,128)(2,1)}, u32[]{:S(2)}, u32[]{:S(2)}) async-start(bf16[1,8,48,2560]{3,2,0,1:T(8,128)(2,1)} %get-tuple-element.61), calls=%async_computation.1 | async-start | bytes 3932160 | tf_op jit(solution)/shard_map/all_to_all | solution.py:84
  71.1 49.0 %all-gather.5.cloned.1.call-done = bf16[1,2560,3072]{2,1,0:T(8,128)(2,1)} async-done(((bf16[1,160,3072]{2,1,0:T(8,128)(2,1)}), bf16[1,2560,3072]{2,1,0:T(8,128)(2,1)}) %all-gather.5.cloned.1.call-update) | async-done | bytes 15728656 | tf_op jit(solution)/shard_map/all_gather | solution.py:79
  120.1 12.2 %fusion.6 = f32[1,384,3072]{2,1,0:T(8,128)} fusion(bf16[384,2560]{1,0:T(8,128)(2,1)S(1)} %bitcast.82, bf16[1,2560,3072]{2,1,0:T(8,128)(2,1)} %all-gather.5.cloned.1.call-done), kind=kOutput, calls=%fused_computation.15 | convolution fusion | flops 6039797760 | bytes 22413312 | tf_op jit(solution)/shard_map/erd,edf->erf/dot_general | solution.py:90
  132.3 10.6 %convolution_convert_fusion.1 = bf16[1536,2560]{1,0:T(8,128)(2,1)} fusion(bf16[384,2560]{1,0:T(8,128)(2,1)} %bitcast.6, f32[384]{0:T(512)S(1)} %reshape.255, f32[1,384,3072]{2,1,0:T(8,128)} %fusion.6), kind=kOutput, calls=%fused_computation.12 | convolution fusion | flops 3027959808 | bytes 14550528 | tf_op jit(solution)/shard_map/erc,erd->ecd/dot_general | solution.py:109
  142.9 82.5 %reduce-scatter.5.cloned.1.call-done = bf16[96,2560]{1,0:T(8,128)(2,1)} async-done(((bf16[1536,2560]{1,0:T(8,128)(2,1)}), bf16[96,2560]{1,0:T(8,128)(2,1)}) %reduce-scatter.5.cloned.1.call-update) | async-done | bytes 491536 | tf_op jit(solution)/shard_map/reduce_scatter | solution.py:115
  225.4 4.5 %multiply_subtract_fusion = (f32[1,96,2560]{2,1,0:T(8,128)}, f32[1,96,2560]{2,1,0:T(8,128)}, f32[1,96,2560]{2,1,0:T(8,128)}, bf16[1,96,2560]{2,1,0:T(8,128)(2,1)}) fusion(f32[1,96,2560]{2,1,0:T(8,128)} %param.19, bf16[96,2560]{1,0:T(8,128)(2,1)} %reduce-scatter.5.cloned.1.call-done, f32[1,96,2560]{2,1,0:T(8,128)} %param.22, f32[1,96,2560]{2,1,0:T(8,128)} %param.25), kind=kLoop, calls=%fused_computation.47 | loop fusion | flops 4177920 | bytes 6881280 | tf_op jit(solution)/shard_map/sub | solution.py:30
  229.9 0.3 reduce-scatter.3.cloned.1.call-start
  230.2 68.9 %all-gather.3.cloned.1.call-done = bf16[1,1536,2560]{2,1,0:T(8,128)(2,1)} async-done(((bf16[1,96,2560]{2,1,0:T(8,128)(2,1)}), bf16[1,1536,2560]{2,1,0:T(8,128)(2,1)}) %all-gather.3.cloned.1.call-update) | async-done | bytes 7864336 | tf_op jit(solution)/shard_map/all_gather | solution.py:80
  299.1 9.1 %fusion.21 = (bf16[384,1536]{1,0:T(8,128)(2,1)S(1)}, bf16[384,1536]{1,0:T(8,128)(2,1)S(1)}, bf16[384]{0:T(512)(128)(2,1)S(1)}) fusion(f32[1,384,3072]{2,1,0:T(8,128)} %fusion.6, f32[384]{0:T(512)S(1)} %reshape.255, bf16[384,2560]{1,0:T(8,128)(2,1)} %bitcast.6, bf16[1,1536,2560]{2,1,0:T(8,128)(2,1)} %all-gather.3.cloned.1.call-done), kind=kOutput, calls=%fused_computation.38 | convolution fusion | flops 3031105024 | bytes 16910592 | tf_op jit(solution)/shard_map/erd,efd->erf/dot_general | solution.py:98
  308.3 1.0 copy-done.8
  309.3 0.4 copy-done.10
  309.7 11.5 %convolution_convert_fusion = bf16[2560,3072]{1,0:T(8,128)(2,1)} fusion(bf16[384,2560]{1,0:T(8,128)(2,1)S(1)} %bitcast.83, bf16[384,1536]{1,0:T(8,128)(2,1)S(1)} %get-tuple-element.54, bf16[384,1536]{1,0:T(8,128)(2,1)S(1)} %get-tuple-element.53), kind=kOutput, calls=%fused_computation.7 | convolution fusion | flops 6052380672 | bytes 20054016 | tf_op jit(solution)/shard_map/erc,erf->ecf/dot_general | solution.py:112
  321.2 0.7 convert_element_type.102
  321.9 5.1 %all-to-all-start.4 = ((bf16[1,8,48]{2,0,1:T(2,128)(2,1)}), bf16[1,8,48]{2,0,1:T(2,128)(2,1)S(1)}, u32[]{:S(2)}, u32[]{:S(2)}) async-start(bf16[1,8,48]{2,0,1:T(2,128)(2,1)} %convert_element_type.102), calls=%async_computation.4 | async-start | bytes 8192 | tf_op jit(solution)/shard_map/all_to_all | solution.py:129
  327.0 11.0 %fusion.9 = bf16[384,2560]{1,0:T(8,128)(2,1)} fusion(bf16[1,2560,3072]{2,1,0:T(8,128)(2,1)} %all-gather.5.cloned.1.call-done, bf16[384,1536]{1,0:T(8,128)(2,1)} %copy-done.10, bf16[384,1536]{1,0:T(8,128)(2,1)S(1)} %copy-done.9), kind=kOutput, calls=%fused_computation.16 | convolution fusion | flops 6045499392 | bytes 20054016 | tf_op jit(solution)/shard_map/erf,edf->erd/dot_general | solution.py:106
  338.0 4.8 %all-to-all-start.3 = ((bf16[1,8,48,2560]{3,2,0,1:T(8,128)(2,1)}), bf16[1,8,48,2560]{3,2,0,1:T(8,128)(2,1)S(1)}, u32[]{:S(2)}, u32[]{:S(2)}) async-start(bf16[1,8,48,2560]{3,2,0,1:T(8,128)(2,1)} %bitcast.84), calls=%async_computation.3 | async-start | bytes 3932160 | tf_op jit(solution)/shard_map/all_to_all | solution.py:122
  342.9 1.9 gather_fusion.3
  344.9 0.2 reshape.253
  345.0 0.6 copy.46
  345.6 22.1 %all-to-all-done.3 = bf16[1,8,48,2560]{3,2,0,1:T(8,128)(2,1)S(1)} async-done(((bf16[1,8,48,2560]{3,2,0,1:T(8,128)(2,1)}), bf16[1,8,48,2560]{3,2,0,1:T(8,128)(2,1)S(1)}, u32[]{:S(2)}, u32[]{:S(2)}) %all-to-all-start.3) | async-done | bytes 1966112 | tf_op jit(solution)/shard_map/all_to_all | solution.py:122
  367.7 2.5 gather_fusion.2
  370.2 3.1 reshape.251
  373.4 4.4 reduce_sum.34
  377.7 48.6 %reduce-scatter.3.cloned.1.call-done = bf16[160,3072]{1,0:T(8,128)(2,1)} async-done(((bf16[2560,3072]{1,0:T(8,128)(2,1)}), bf16[160,3072]{1,0:T(8,128)(2,1)}) %reduce-scatter.3.cloned.1.call-update) | async-done | bytes 983056 | tf_op jit(solution)/shard_map/reduce_scatter | solution.py:118
  426.3 1.4 bitcast_convert_fusion
  427.8 5.8 %multiply_subtract_fusion.1 = (f32[1,160,1536]{2,1,0:T(8,128)}, f32[1,160,1536]{2,1,0:T(8,128)}, f32[1,160,1536]{2,1,0:T(8,128)}, f32[1,160,1536]{2,1,0:T(8,128)...) fusion(f32[1,160,1536]{2,1,0:T(8,128)S(1)} %copy-done.3, f32[1,160,3072]{2,1,0:T(8,128)S(1)} %bitcast_convert_fusion, ...), kind=kLoop, calls=%fused_computation.48 | loop fusion | flops 7372800 | bytes 13762560 | tf_op jit(solution)/shard_map/sub | solution.py:30
  (46 shorter events, 0.6 us)
Async XLA Ops:
  7.2 18.3 %copy-start = (bf16[128,2560]{1,0:T(8,128)(2,1)S(1)}, bf16[128,2560]{1,0:T(8,128)(2,1)}, u32[]{:S(2)}) copy-start(bf16[128,2560]{1,0:T(8,128)(2,1)} %param.13) | copy-start | bytes 1966084
  7.2 112.9 %all-gather.5.cloned.1.call-start = ((), (), s32[]{:S(2)}) async-start(), calls=%async_computation.8 | async-start | bytes 16711680 | tf_op jit(solution)/shard_map/all_gather | solution.py:79
  8.6 2.4 copy-start.6
  8.6 3.9 copy-start.7
  15.7 20.2 %all-to-all-start = ((bf16[1,8,48]{2,0,1:T(2,128)(2,1)}), bf16[1,8,48]{2,0,1:T(2,128)(2,1)S(1)}, u32[]{:S(2)}, u32[]{:S(2)}) async-start(bf16[1,8,48]{2,0,1:T(2,128)(2,1)} %reshape.315), calls=%async_computation | async-start | bytes 8192 | tf_op jit(solution)/shard_map/all_to_all | solution.py:85
  25.5 3.3 copy-start.2
  65.8 54.3 %copy-start.5 = (bf16[1,8,48,2560]{3,2,0,1:T(8,128)(2,1)S(1)}, bf16[1,8,48,2560]{3,2,0,1:T(8,128)(2,1)}, u32[]{:S(2)}) copy-start(bf16[1,8,48,2560]{3,2,0,1:T(8,128)(2,1)} %all_to_all.25) | copy-start | bytes 5898244
  65.8 66.5 %all-to-all-start.1 = ((bf16[1,8,48,2560]{3,2,0,1:T(8,128)(2,1)}), bf16[1,8,48,2560]{3,2,0,1:T(8,128)(2,1)}, u32[]{:S(2)}, u32[]{:S(2)}) async-start(bf16[1,8,48,2560]{3,2,0,1:T(8,128)(2,1)} %get-tuple-element.61), calls=%async_computation.1 | async-start | bytes 3932160 | tf_op jit(solution)/shard_map/all_to_all | solution.py:84
  71.0 154.4 %reduce-scatter.5.cloned.1.call-start = ((), (), s32[]{:S(2)}) async-start(), calls=%async_computation.10 | async-start | bytes 8355840 | tf_op jit(solution)/shard_map/reduce_scatter | solution.py:115
  142.8 156.3 %all-gather.3.cloned.1.call-start = ((), (), s32[]{:S(2)}) async-start(), calls=%async_computation.7 | async-start | bytes 8355840 | tf_op jit(solution)/shard_map/all_gather | solution.py:80
  229.9 196.4 %reduce-scatter.3.cloned.1.call-start = ((), (), s32[]{:S(2)}) async-start(), calls=%async_computation.9 | async-start | bytes 16711680 | tf_op jit(solution)/shard_map/reduce_scatter | solution.py:118
  308.3 1.0 copy-start.8
  308.3 1.4 copy-start.10
  321.2 5.8 %copy-start.9 = (bf16[384,1536]{1,0:T(8,128)(2,1)S(1)}, bf16[384,1536]{1,0:T(8,128)(2,1)}, u32[]{:S(2)}) copy-start(bf16[384,1536]{1,0:T(8,128)(2,1)} %copy-done.8) | copy-start | bytes 3538948
  321.9 16.1 %all-to-all-start.4 = ((bf16[1,8,48]{2,0,1:T(2,128)(2,1)}), bf16[1,8,48]{2,0,1:T(2,128)(2,1)S(1)}, u32[]{:S(2)}, u32[]{:S(2)}) async-start(bf16[1,8,48]{2,0,1:T(2,128)(2,1)} %convert_element_type.102), calls=%async_computation.4 | async-start | bytes 8192 | tf_op jit(solution)/shard_map/all_to_all | solution.py:129
  338.0 29.7 %all-to-all-start.3 = ((bf16[1,8,48,2560]{3,2,0,1:T(8,128)(2,1)}), bf16[1,8,48,2560]{3,2,0,1:T(8,128)(2,1)S(1)}, u32[]{:S(2)}, u32[]{:S(2)}) async-start(bf16[1,8,48,2560]{3,2,0,1:T(8,128)(2,1)} %bitcast.84), calls=%async_computation.3 | async-start | bytes 3932160 | tf_op jit(solution)/shard_map/all_to_all | solution.py:122
  373.4 54.4 %copy-start.3 = (f32[1,160,1536]{2,1,0:T(8,128)S(1)}, f32[1,160,1536]{2,1,0:T(8,128)}, u32[]{:S(2)}) copy-start(f32[1,160,1536]{2,1,0:T(8,128)} %param.18) | copy-start | bytes 2949124
  377.7 50.0 %copy-start.4 = (f32[1,160,1536]{2,1,0:T(8,128)S(1)}, f32[1,160,1536]{2,1,0:T(8,128)}, u32[]{:S(2)}) copy-start(f32[1,160,1536]{2,1,0:T(8,128)} %param.17) | copy-start | bytes 2949124
  427.8 5.8 %copy-start.1 = (bf16[128,2560]{1,0:T(8,128)(2,1)S(1)}, bf16[128,2560]{1,0:T(8,128)(2,1)}, u32[]{:S(2)}) copy-start(bf16[128,2560]{1,0:T(8,128)(2,1)} %param.13) | copy-start | bytes 1966084
Sparse Core Ops, SparseCore 0:
  11.0 108.9 all-gather.4
  143.0 82.4 reduce-scatter.4
  230.1 69.0 all-gather.2
  321.3 104.9 reduce-scatter.2

commit v2 on v1

v2 whole, which is shorter than its diff:
```python
import jax
import jax.numpy as jnp
from jax import lax
from jax.experimental import pallas as pl
from jax.experimental.pallas import tpu as pltpu
from jax.sharding import Mesh
from jax.sharding import PartitionSpec as P

beta_one = 0.9
beta_two = 0.95
learn_rate = 0.003
decay_rate = 0.1
epsilon = 1e-08
correct_one = 1.0 - 2.6561398887587e-05
correct_two = 1.0 - 0.005920529220333

LANES = 128
GROUPS = 8
f32 = jnp.float32
bf16 = jnp.bfloat16

PLUS = [(i, (i + 1) % 4) for i in range(4)]
MINUS = [(i, (i - 1) % 4) for i in range(4)]
SWAP = [(0, 1), (1, 0)]
PAIR_A = [(2 * yl + c, 2 * c + yl) for yl in range(2) for c in range(2)]
PAIR_B = [(2 * yl + c, 2 * c + 1 - yl) for yl in range(2) for c in range(2)]


def _cycle():
    pairs = []
    for x1 in range(2):
        for x0 in range(2):
            for yh in range(2):
                for yl in range(2):
                    for c in range(2):
                        src = (((x1 * 2 + x0) * 2 + yh) * 2 + yl) * 2 + c
                        dst = (((x1 * 2 + yh) * 2 + yl) * 2 + c) * 2 + x0
                        pairs.append((src, dst))
    return pairs


CYCLE = _cycle()
CYCLE_AXES = ("x", "yh", "yl", "c")


def back(pairs):
    return [(d, s) for s, d in pairs]


def piece_pairs(piece):
    db, dz = piece // 4, piece % 4
    return [
        (yl * 4 + z, (yl ^ db) * 4 + (z + dz) % 4) for yl in range(2) for z in range(4)
    ]


def adamw(weight, moment, second, grad):
    moment_new = beta_one * moment + (1.0 - beta_one) * grad
    second_new = beta_two * second + (1.0 - beta_two) * grad * grad
    update = moment_new / correct_one / (jnp.sqrt(second_new / correct_two) + epsilon)
    return (weight - learn_rate * (update + decay_rate * weight), moment_new, second_new)


def one_hots(place_ref, ids, capacity):
    tok = ids.shape[1]
    experts = lax.broadcasted_iota(jnp.int32, (GROUPS, tok), 0)
    named = [(experts == ids[k : k + 1, :]).astype(f32) for k in range(2)]
    earlier = (
        lax.broadcasted_iota(jnp.int32, (tok, tok), 0)
        < lax.broadcasted_iota(jnp.int32, (tok, tok), 1)
    ).astype(f32)
    count = jnp.dot(
        (named[0] + named[1]).astype(bf16), earlier.astype(bf16), preferred_element_type=f32
    )
    slot = lax.broadcasted_iota(jnp.int32, (GROUPS * capacity, tok), 0)
    hots = []
    for k in range(2):
        rank = jnp.sum(named[k] * count, axis=0, keepdims=True).astype(jnp.int32)
        expert = ids[k : k + 1, :]
        db = (expert + place_ref[0]) & 1
        dz = ((expert >> 1) + 4 - place_ref[1]) & 3
        dest = (db * 4 + dz) * capacity + rank
        hots.append((slot == dest).astype(f32))
    return hots


def pack_kernel(capacity, width, place_ref, ids_ref, probs_ref, x_ref, y_ref, *out_refs):
    first, second = one_hots(place_ref, ids_ref[...], capacity)
    hot = (first + second).astype(bf16)
    probs = probs_ref[...]
    gates = (first * probs[0:1, :] + second * probs[1:2, :]).astype(bf16)
    ones = jnp.ones((gates.shape[1], LANES), bf16)
    x_rows = jnp.dot(hot, x_ref[...], preferred_element_type=f32).astype(bf16)
    for k in range(GROUPS):
        out_refs[k][:, :width] = x_rows[k * capacity : (k + 1) * capacity]
    y_rows = jnp.dot(hot, y_ref[...], preferred_element_type=f32).astype(bf16)
    for k in range(GROUPS):
        out_refs[k][:, width : 2 * width] = y_rows[k * capacity : (k + 1) * capacity]
    g_rows = jnp.dot(gates, ones, preferred_element_type=f32).astype(bf16)
    for k in range(GROUPS):
        out_refs[k][:, 2 * width :] = g_rows[k * capacity : (k + 1) * capacity]


def unpack_kernel(capacity, width, place_ref, ids_ref, *refs):
    in_refs, x_ref, prob_ref, rows_ref = refs[:GROUPS], refs[-3], refs[-2], refs[-1]
    for k in range(GROUPS):
        rows_ref[k * capacity : (k + 1) * capacity, :] = in_refs[k][...]
    first, second = one_hots(place_ref, ids_ref[...], capacity)
    hot = (first + second).astype(bf16)
    x_ref[...] = lax.dot_general(
        hot, rows_ref[:, :width], (((0,), (0,)), ((), ())), preferred_element_type=f32
    ).astype(bf16)
    q_col = rows_ref[:, width:].astype(f32)
    prob_ref[0:1, :] = jnp.sum(first * q_col, axis=0, keepdims=True).astype(bf16)
    prob_ref[1:2, :] = jnp.sum(second * q_col, axis=0, keepdims=True).astype(bf16)


def vmem_specs(count):
    return [pl.BlockSpec(memory_space=pltpu.VMEM) for _ in range(count)]


def pack_rows(place, ids, probs, x, y, capacity):
    width = x.shape[1]
    piece = jax.ShapeDtypeStruct((capacity, 2 * width + LANES), bf16)
    return pl.pallas_call(
        lambda *refs: pack_kernel(capacity, width, *refs),
        out_shape=(piece,) * GROUPS,
        in_specs=[pl.BlockSpec(memory_space=pltpu.SMEM)] + vmem_specs(4),
        out_specs=tuple(vmem_specs(GROUPS)),
        compiler_params=pltpu.CompilerParams(vmem_limit_bytes=40 << 20),
        name="pack_rows",
    )(place, ids, probs, x, y)


def unpack_rows(place, ids, pieces, width, capacity):
    tok = ids.shape[1]
    return pl.pallas_call(
        lambda *refs: unpack_kernel(capacity, width, *refs),
        out_shape=(
            jax.ShapeDtypeStruct((tok, width), bf16),
            jax.ShapeDtypeStruct((2, tok), bf16),
        ),
        in_specs=[pl.BlockSpec(memory_space=pltpu.SMEM)] + vmem_specs(1 + GROUPS),
        out_specs=tuple(vmem_specs(2)),
        scratch_shapes=[pltpu.VMEM((GROUPS * capacity, width + LANES), bf16)],
        compiler_params=pltpu.CompilerParams(vmem_limit_bytes=40 << 20),
        name="unpack_rows",
    )(place, ids, *pieces)


def put(whole, part, row):
    return lax.dynamic_update_slice(whole, part, (row, 0))


def ring(part, half):
    left = lax.ppermute(part, "x", PLUS)
    right = lax.ppermute(part, "x", MINUS)
    far_top = lax.ppermute(left[:half], "x", PLUS)
    far_low = lax.ppermute(right[half:], "x", MINUS)
    return left, right, far_top, far_low


def gather_gate_up(part, x, yh):
    size = part.shape[0]
    other = lax.ppermute(part, "yh", SWAP)
    whole = jnp.zeros((8 * size, part.shape[1]), part.dtype)
    for piece, side in ((part, yh), (other, 1 - yh)):
        left, right, far_top, far_low = ring(piece, size // 2)

        def row(k):
            return size * (2 * ((x + k) % 4) + side)

        whole = put(whole, piece, row(0))
        whole = put(whole, left, row(3))
        whole = put(whole, right, row(1))
        whole = put(whole, far_top, row(2))
        whole = put(whole, far_low, row(2) + size // 2)
    return whole


def gather_down(part, x, yh):
    size = part.shape[0]
    other = lax.ppermute(part, "yh", SWAP)
    both = jnp.where(
        yh == 0, jnp.concatenate((part, other)), jnp.concatenate((other, part))
    )
    left, right, far_top, far_low = ring(both, size)
    whole = jnp.zeros((8 * size, part.shape[1]), part.dtype)
    for k, piece in ((0, both), (3, left), (1, right)):
        whole = put(whole, piece, 2 * size * ((x + k) % 4))
    whole = put(whole, far_top, 2 * size * ((x + 2) % 4))
    return put(whole, far_low, 2 * size * ((x + 2) % 4) + size)


def scatter_sum(terms, x, yh):
    size, n = terms.shape[0] // 8, terms.shape[1]

    def rows(k, side, count):
        return lax.dynamic_slice(
            terms, (size * (2 * ((x + k) % 4) + side), 0), (count * size, n)
        )

    def plus(*values):
        return sum(v.astype(f32) for v in values).astype(bf16)

    from_left = lax.ppermute(rows(2, 0, 1), "x", PLUS)
    from_right = lax.ppermute(rows(2, 1, 1), "x", MINUS)
    to_right = jnp.concatenate((plus(rows(1, 0, 1), from_left), rows(1, 1, 1)))
    to_left = jnp.concatenate((rows(3, 0, 1), plus(rows(3, 1, 1), from_right)))
    from_left = lax.ppermute(to_right, "x", PLUS)
    from_right = lax.ppermute(to_left, "x", MINUS)

    def mine(side):
        cut = lambda v: lax.dynamic_slice(v, (size * side, 0), (size, n))
        return plus(rows(0, side, 1), cut(from_left), cut(from_right))

    sent = lax.ppermute(mine(1 - yh), "yh", SWAP)
    return plus(mine(yh), sent)


def body(
    layer_input,
    output_grad,
    expert_ids,
    gate_probs,
    gate_weight,
    up_weight,
    down_weight,
    gate_moment,
    up_moment,
    down_moment,
    gate_second,
    up_second,
    down_second,
):
    x, yh, yl = lax.axis_index("x"), lax.axis_index("yh"), lax.axis_index("yl")
    z, c = lax.axis_index("z"), lax.axis_index("c")
    tok, picks = expert_ids.shape
    capacity = 3 * tok * picks // (2 * GROUPS)
    width = layer_input.shape[1]
    hidden_units = gate_weight.shape[2]
    quarter = hidden_units // 4
    half = hidden_units // 2
    rows = GROUPS * capacity

    gate_low, up_low = gate_weight[0].astype(bf16), up_weight[0].astype(bf16)

    def chunk(core):
        cuts = [
            w[:, (core + 2 * k) * quarter : (core + 2 * k + 1) * quarter]
            for w in (gate_low, up_low)
            for k in range(2)
        ]
        return jnp.concatenate(cuts, axis=1)

    chunks = (chunk(0), chunk(1))
    part_a = lax.ppermute(jnp.where(yl == 0, chunks[0], chunks[1]), ("yl", "c"), PAIR_A)
    part_b = lax.ppermute(jnp.where(yl == 0, chunks[1], chunks[0]), ("yl", "c"), PAIR_B)
    part = jnp.where(
        c == 0, jnp.concatenate((part_a, part_b)), jnp.concatenate((part_b, part_a))
    )
    down_part = lax.ppermute(down_weight[0].astype(bf16), CYCLE_AXES, CYCLE)
    w_gate_up = gather_gate_up(part, x, yh)
    w_down = gather_down(down_part, x, yh)

    place = jnp.stack((yl, z)).astype(jnp.int32)
    ids = expert_ids.T
    sent = pack_rows(place, ids, gate_probs.T.astype(f32), layer_input, output_grad, capacity)
    got = [sent[0]] + [
        lax.ppermute(sent[k], ("yl", "z"), piece_pairs(k)) for k in range(1, GROUPS)
    ]
    own = jnp.concatenate(got)
    other = lax.ppermute(own, "c", SWAP)
    x_rows = jnp.concatenate((own[:, :width], other[:, :width]))
    y_rows = jnp.concatenate((own[:, width : 2 * width], other[:, width : 2 * width]))
    gates = jnp.concatenate((own[:, 2 * width :], other[:, 2 * width :]))[:, :1].astype(f32)

    pre = jnp.dot(x_rows, w_gate_up, preferred_element_type=f32)
    gate_pre, up_pre = pre[:, :half], pre[:, half:]
    sigmoid_gate = jax.nn.sigmoid(gate_pre)
    silu_gate = gate_pre * sigmoid_gate
    hidden_full = silu_gate * up_pre
    hidden = hidden_full.astype(bf16)
    hidden_scaled = (gates * hidden_full).astype(bf16)
    down_term = lax.dot_general(
        hidden_scaled, y_rows, (((0,), (0,)), ((), ())), preferred_element_type=f32
    ).astype(bf16)
    grad_down = scatter_sum(down_term, x, yh)
    raw_grad = lax.dot_general(
        y_rows, w_down, (((1,), (1,)), ((), ())), preferred_element_type=f32
    )
    prob_rows = jnp.sum(hidden.astype(f32) * raw_grad, axis=1, keepdims=True)
    hidden_grad = gates * raw_grad
    dsilu = sigmoid_gate * (1.0 + gate_pre * (1.0 - sigmoid_gate))
    pre_grad = jnp.concatenate(
        (hidden_grad * up_pre * dsilu, hidden_grad * silu_gate), axis=1
    ).astype(bf16)
    gate_up_term = lax.dot_general(
        x_rows, pre_grad, (((0,), (0,)), ((), ())), preferred_element_type=f32
    ).astype(bf16)
    grad_gate_up = scatter_sum(gate_up_term, x, yh)

    def input_part(d_rows):
        return lax.dot_general(
            d_rows, w_gate_up, (((1,), (1,)), ((), ())), preferred_element_type=f32
        )

    far_rows = lax.ppermute(input_part(pre_grad[rows:]).astype(bf16), "c", SWAP)
    far_prob = lax.ppermute(
        jnp.broadcast_to(prob_rows[rows:], (rows, LANES)), "c", SWAP
    )
    near_rows = (input_part(pre_grad[:rows]) + far_rows.astype(f32)).astype(bf16)
    near_prob = (prob_rows[:rows] + far_prob).astype(bf16)
    packed = jnp.concatenate((near_rows, near_prob), axis=1)
    pieces = [packed[k * capacity : (k + 1) * capacity] for k in range(GROUPS)]
    returned = [pieces[0]] + [
        lax.ppermute(pieces[k], ("yl", "z"), back(piece_pairs(k))) for k in range(1, GROUPS)
    ]
    input_grad, prob_grad = unpack_rows(place, ids, returned, width, capacity)

    depth = gate_weight.shape[1]
    home_a = lax.ppermute(
        lax.dynamic_slice(grad_gate_up, (depth * c, 0), (depth, hidden_units)),
        ("yl", "c"),
        back(PAIR_A),
    ).astype(f32)
    home_b = lax.ppermute(
        lax.dynamic_slice(grad_gate_up, (depth * (1 - c), 0), (depth, hidden_units)),
        ("yl", "c"),
        back(PAIR_B),
    ).astype(f32)
    grad_down = lax.ppermute(grad_down, CYCLE_AXES, back(CYCLE)).astype(f32)
    even = jnp.where(yl == 0, home_a, home_b)
    odd = jnp.where(yl == 0, home_b, home_a)

    def natural(start):
        return jnp.concatenate(
            [
                v[:, start + k * quarter : start + (k + 1) * quarter]
                for k in range(2)
                for v in (even, odd)
            ],
            axis=1,
        )[None]

    new_gate_weight, new_gate_moment, new_gate_second = adamw(
        gate_weight, gate_moment, gate_second, natural(0)
    )
    new_up_weight, new_up_moment, new_up_second = adamw(
        up_weight, up_moment, up_second, natural(half)
    )
    new_down_weight, new_down_moment, new_down_second = adamw(
        down_weight, down_moment, down_second, grad_down[None]
    )
    return (
        input_grad,
        prob_grad.T,
        new_gate_weight,
        new_up_weight,
        new_down_weight,
        new_gate_moment,
        new_up_moment,
        new_down_moment,
        new_gate_second,
        new_up_second,
        new_down_second,
    )


def solution(mesh):
    fine = Mesh(mesh.devices.reshape(4, 2, 2, 4, 2), ("x", "yh", "yl", "z", "c"))
    tokens = P(("x", "yh", "yl", "z", "c"), None)
    weights = P(("z", "c"), ("x", "yh", "yl"), None)
    return jax.shard_map(
        body,
        mesh=fine,
        in_specs=(tokens,) * 4 + (weights,) * 9,
        out_specs=(tokens,) * 2 + (weights,) * 9,
        check_vma=False,
    )
```

time: 441 us -> 499 us (1.13); the launches traced: 440 us -> 489 us
  starting transfers between devices: 22.3 us -> 109 us
  blocking collectives: 29.9 us -> 0 us
  local copies, waits for them, and re-layouts: 24.1 us -> 50.1 us
  waiting for transfers between devices: 271 us -> 248 us
  between operations: 14 us -> 1.69 us
  matrix products: 54.4 us -> 44.7 us
  other arithmetic: 24.3 us -> 30.2 us
    ppermute x0 -> x47, waiting for transfers between devices: none -> 248 us  [the longest x3 51.9 us: ring(): left = lax.ppermute(part, 'x', PLUS)]
    reduce_scatter x2 -> x0, waiting for transfers between devices: 131 us -> none  [the longest x1 82.5 us: body(): lax.psum_scatter(second[0], 'dp', scatter_dimension=0, tiled=True)[None]]
    all_gather x2 -> x0, waiting for transfers between devices: 118 us -> none  [the longest x1 68.9 us: body(): lax.all_gather(w_down_shard, 'dp', axis=1, tiled=True)]
    ppermute x0 -> x47, starting transfers between devices: none -> 109 us  [the longest x1 16.1 us: body(): lax.ppermute(lax.dynamic_slice(grad_gate_up, (depth * c, 0), (depth, hidd...]
    all_to_all x1 -> x0, blocking collectives: 29.9 us -> none  [body(): lax.all_to_all(send_input, 'expert', split_axis=1, concat_axis=1, tiled=T...]
    all_to_all x4 -> x0, waiting for transfers between devices: 22.1 us -> none  [the longest x1 22.1 us: body(): lax.all_to_all(input_rows.reshape(exp_dev, groups, capacity, width), 'exp...]
    all_to_all x4 -> x0, starting transfers between devices: 21.9 us -> none  [the longest x1 6.81 us: body(): lax.all_to_all(send_gate, 'expert', split_axis=1, concat_axis=1, tiled=True)]
    unnamed x25 -> x67, local copies, waits for them, and re-layouts: 2.33 us -> 21.2 us
  transfers between devices with their start and end apart: 8 -> 47, of which waited for: 5 -> 27; matrix products, arithmetic and copies ran while one was open for 12% -> 12% of each run, Pallas kernels for 0% -> 0%
where the time goes in v2:
time: 499 us; the launch traced here: 489 us
  waiting for transfers between devices  248 us (50%)
  starting transfers between devices  109 us (22%)
  local copies, waits for them, and re-layouts  50.1 us (10%)
  matrix products  44.7 us (9%)
  other arithmetic  30.2 us (6%)
    ppermute x3, waiting for transfers between devices, ring(): left = lax.ppermute(part, 'x', PLUS)  51.9 us
    ppermute x2, waiting for transfers between devices, scatter_sum(): from_left = lax.ppermute(to_right, 'x', PLUS)  35.4 us
    ppermute x7, waiting for transfers between devices, body(): lax.ppermute(sent[k], ('yl', 'z'), piece_pairs(k))  32.4 us
    ppermute x7, waiting for transfers between devices, body(): lax.ppermute(pieces[k], ('yl', 'z'), back(piece_pairs(k)))  26.5 us
    ppermute x2, waiting for transfers between devices, scatter_sum(): from_left = lax.ppermute(rows(2, 0, 1), 'x', PLUS)  24.7 us
    unnamed x67, local copies, waits for them, and re-layouts  21.2 us
    ppermute x1, waiting for transfers between devices, body(): grad_down = lax.ppermute(grad_down, CYCLE_AXES, back(CYCLE)).astype(f32)  18.3 us
    ppermute x1, starting transfers between devices, body(): lax.ppermute(lax.dynamic_slice(grad_gate_up, (depth * c, 0), (depth, hidd...  16.1 us
  transfers between devices with their start and end apart: 47, of which 27 were waited for; matrix products, arithmetic and copies ran while one was open for 12% of the time, Pallas kernels for 0%

profile of v2, /device:TPU:1, one launch (start us, length us, event | category | flops | bytes accessed | tf_op | source)
XLA Modules:
  0.0 489.1 jit_solution(701107002619887307)
XLA Ops:
  4.2 2.6 pack_rows.1
  9.4 3.3 collective-permute-start.1
  20.4 2.6 collective-permute-done
  27.3 23.5 %collective-permute-done.1 = bf16[48,5248]{1,0:T(8,128)(2,1)} collective-permute-done((bf16[48,5248]{1,0:T(8,128)(2,1)S(1)}, bf16[48,5248]{1,0:T(8,128)(2,1)}, u32[]{:S(2)}, u32[]{:S(2)}) %collective-permute-start.1) | collective-permute-done | bytes 503840 | tf_op jit(solution)/shard_map/ppermute | solution.py:270
  59.1 6.3 %collective-permute-done.6 = bf16[48,5248]{1,0:T(8,128)(2,1)S(1)} collective-permute-done((bf16[48,5248]{1,0:T(8,128)(2,1)S(1)}, bf16[48,5248]{1,0:T(8,128)(2,1)S(1)}, u32[]{:S(2)}, u32[]{:S(2)}) %collective-permute-start.6) | collective-permute-done | bytes 503840 | tf_op jit(solution)/shard_map/ppermute | solution.py:270
  66.2 3.9 collective-permute-start.7
  70.3 2.8 collective-permute-start.14
  73.2 7.2 %collective-permute-done.14 = bf16[160,1536]{1,0:T(8,128)(2,1)S(1)} collective-permute-done((bf16[160,1536]{1,0:T(8,128)(2,1)S(1)}, bf16[160,1536]{1,0:T(8,128)(2,1)S(1)}, u32[]{:S(2)}, u32[]{:S(2)}) %collective-permute-start.14) | collective-permute-done | bytes 491552 | tf_op jit(solution)/shard_map/ppermute | solution.py:257
  80.5 3.7 collective-permute-done.15
  84.1 3.6 broadcast_in_dim.7
  92.0 2.8 collective-permute-start.20
  98.0 13.6 %collective-permute-done.16 = bf16[320,1536]{1,0:T(8,128)(2,1)S(1)} collective-permute-done((bf16[320,1536]{1,0:T(8,128)(2,1)}, bf16[320,1536]{1,0:T(8,128)(2,1)S(1)}, u32[]{:S(2)}, u32[]{:S(2)}) %collective-permute-start.16) | collective-permute-done | bytes 983072 | tf_op jit(solution)/shard_map/ppermute | solution.py:156
  111.9 2.7 collective-permute-start.19
  114.6 2.7 collective-permute-start.22
  119.3 3.2 collective-permute-done.18
  125.2 18.4 %collective-permute-done.21 = bf16[320,1536]{1,0:T(8,128)(2,1)S(1)} collective-permute-done((bf16[320,1536]{1,0:T(8,128)(2,1)S(1)}, bf16[320,1536]{1,0:T(8,128)(2,1)S(1)}, u32[]{:S(2)}, u32[]{:S(2)}) %collective-permute-start.21) | collective-permute-done | bytes 983072 | tf_op jit(solution)/shard_map/ppermute | solution.py:156
  143.8 2.9 collective-permute-start.24
  148.7 4.8 collective-permute-done.23
  158.6 10.1 %fusion.1 = f32[768,1536]{0,1:T(8,128)S(1)} fusion(bf16[2560,1536]{1,0:T(8,128)(2,1)} %constant_dynamic-update-slice_fusion.8, bf16[384,2560]{1,0:T(8,128)(2,1)S(1)} %get-tuple-element.56, bf16[384,2560]{1,0:T(8,128)(2,1)S(1)} %get-tuple-element.54), kind=kOutput, calls=%fused_computation.19 | convolution fusion | flops 6047662080 | bytes 16515072 | tf_op jit(solution)/shard_map/dot_general | solution.py:278
  168.8 3.3 convolution_convert_fusion.1
  174.2 2.7 collective-permute-start.43
  176.8 6.2 %collective-permute-done.41 = bf16[96,2560]{1,0:T(8,128)(2,1)S(1)} collective-permute-done((bf16[96,2560]{1,0:T(8,128)(2,1)S(1)}, bf16[96,2560]{1,0:T(8,128)(2,1)S(1)}, u32[]{:S(2)}, u32[]{:S(2)}) %collective-permute-start.41) | collective-permute-done | bytes 491552 | tf_op jit(solution)/shard_map/ppermute | solution.py:206
  189.2 14.9 %collective-permute-done.42 = bf16[192,2560]{1,0:T(8,128)(2,1)} collective-permute-done((bf16[192,2560]{1,0:T(8,128)(2,1)}, bf16[192,2560]{1,0:T(8,128)(2,1)}, u32[]{:S(2)}, u32[]{:S(2)}) %collective-permute-start.42) | collective-permute-done | bytes 983072 | tf_op jit(solution)/shard_map/ppermute | solution.py:210
  206.4 2.8 collective-permute-start.45
  209.2 6.6 %collective-permute-done.45 = bf16[96,2560]{1,0:T(8,128)(2,1)S(1)} collective-permute-done((bf16[96,2560]{1,0:T(8,128)(2,1)}, bf16[96,2560]{1,0:T(8,128)(2,1)S(1)}, u32[]{:S(2)}, u32[]{:S(2)}) %collective-permute-start.45) | collective-permute-done | bytes 491552 | tf_op jit(solution)/shard_map/ppermute | solution.py:217
  217.4 11.9 %collective-permute-start.46 = (bf16[96,2560]{1,0:T(8,128)(2,1)S(1)}, bf16[96,2560]{1,0:T(8,128)(2,1)S(1)}, u32[]{:S(2)}, u32[]{:S(2)}) collective-permute-start(bf16[96,2560]{1,0:T(8,128)(2,1)S(1)} %add_convert_fusion.5), channel_id=1, source_target_pairs={{0,0},{8,1},{16,8},{24,9},{32,16},{40,17},{48,24},{56,25},{1,32},{... | collective-permute-start | bytes 1474568 | tf_op jit(solution)/shard_map/ppermute | solution.py:332
  229.3 18.3 %collective-permute-done.46 = bf16[96,2560]{1,0:T(8,128)(2,1)S(1)} collective-permute-done((bf16[96,2560]{1,0:T(8,128)(2,1)S(1)}, bf16[96,2560]{1,0:T(8,128)(2,1)S(1)}, u32[]{:S(2)}, u32[]{:S(2)}) %collective-permute-start.46) | collective-permute-done | bytes 491552 | tf_op jit(solution)/shard_map/ppermute | solution.py:332
  249.8 9.5 %collective-permute-start.8 = (bf16[96,2560]{1,0:T(8,128)(2,1)S(1)}, bf16[96,2560]{1,0:T(8,128)(2,1)S(1)}, u32[]{:S(2)}, u32[]{:S(2)}) collective-permute-start(bf16[96,2560]{1,0:T(8,128)(2,1)S(1)} %get-tuple-element.71), channel_id=1, source_target_pairs={{0,0},{1,8},{8,16},{9,24},{16,32},{17,40},{24,48},{25,56},{32,1},{... | collective-permute-start | bytes 1474568 | tf_op jit(solution)/shard_map/ppermute | solution.py:262
  259.2 8.8 %collective-permute-done.8 = bf16[96,2560]{1,0:T(8,128)(2,1)S(1)} collective-permute-done((bf16[96,2560]{1,0:T(8,128)(2,1)S(1)}, bf16[96,2560]{1,0:T(8,128)(2,1)S(1)}, u32[]{:S(2)}, u32[]{:S(2)}) %collective-permute-start.8) | collective-permute-done | bytes 491552 | tf_op jit(solution)/shard_map/ppermute | solution.py:262
  269.7 11.6 %collective-permute-done.9 = bf16[96,2560]{1,0:T(8,128)(2,1)S(1)} collective-permute-done((bf16[96,2560]{1,0:T(8,128)(2,1)S(1)}, bf16[96,2560]{1,0:T(8,128)(2,1)S(1)}, u32[]{:S(2)}, u32[]{:S(2)}) %collective-permute-start.9) | collective-permute-done | bytes 491552 | tf_op jit(solution)/shard_map/ppermute | solution.py:183
  284.6 2.7 collective-permute-start.11
  287.3 19.9 %collective-permute-done.10 = bf16[192,2560]{1,0:T(8,128)(2,1)S(1)} collective-permute-done((bf16[192,2560]{1,0:T(8,128)(2,1)S(1)}, bf16[192,2560]{1,0:T(8,128)(2,1)S(1)}, u32[]{:S(2)}, u32[]{:S(2)}) %collective-permute-start.10) | collective-permute-done | bytes 983072 | tf_op jit(solution)/shard_map/ppermute | solution.py:156
  312.3 6.3 %collective-permute-done.12 = bf16[96,2560]{1,0:T(8,128)(2,1)S(1)} collective-permute-done((bf16[96,2560]{1,0:T(8,128)(2,1)S(1)}, bf16[96,2560]{1,0:T(8,128)(2,1)S(1)}, u32[]{:S(2)}, u32[]{:S(2)}) %collective-permute-start.12) | collective-permute-done | bytes 491552 | tf_op jit(solution)/shard_map/ppermute | solution.py:158
  320.5 7.9 %multiply_convert_fusion.1 = (bf16[768,768]{0,1:T(8,128)(2,1)S(1)}, bf16[768,768]{0,1:T(8,128)(2,1)S(1)}, f32[768]{0:T(1024)S(1)}) fusion(f32[768]{0:T(1024)S(1)} %convert_reduce_fusion, f32[768,1536]{0,1:T(8,128)} %copy-done.29, bf16[768,2560]{1,0:T(8,128)(2,1)} %constant_dynamic-update-slice_fusion.18, bf16[384,2560]{1,0:T(8,128)(2,1)S(1)} %copy-done.16, ...), kind=kOutput, calls=%fused_computation.23 | convolution fusion | flops 3038969088 | bytes 14948352 | tf_op jit(solution)/shard_map/dot_general | solution.py:289
  328.4 8.1 %convolution_convert_fusion = bf16[2560,1536]{1,0:T(8,128)(2,1)S(1)} fusion(bf16[384,2560]{1,0:T(8,128)(2,1)S(1)} %copy-done.14, bf16[384,2560]{1,0:T(8,128)(2,1)S(1)} %copy-done.10, bf16[768,768]{0,1:T(8,128)(2,1)S(1)} %get-tuple-element.50, bf16[768,768]{0,1:T(8,128)(2,1)S(1)} %get-tuple-element.51), kind=kOutput, calls=%fused_computation | convolution fusion | flops 6056312832 | bytes 14155776 | tf_op jit(solution)/shard_map/dot_general | solution.py:298
  343.1 18.5 %collective-permute-done.34 = bf16[320,1536]{1,0:T(8,128)(2,1)S(1)} collective-permute-done((bf16[320,1536]{1,0:T(8,128)(2,1)}, bf16[320,1536]{1,0:T(8,128)(2,1)S(1)}, u32[]{:S(2)}, u32[]{:S(2)}) %collective-permute-start.34) | collective-permute-done | bytes 983072 | tf_op jit(solution)/shard_map/ppermute | solution.py:206
  362.5 2.6 add_convert_fusion.4
  370.7 7.9 %convolution_convert_fusion.2 = bf16[384,2560]{1,0:T(8,128)(2,1)} fusion(bf16[2560,1536]{1,0:T(8,128)(2,1)} %constant_dynamic-update-slice_fusion.8, bf16[768,768]{0,1:T(8,128)(2,1)S(1)} %copy-done.28, bf16[768,768]{0,1:T(8,128)(2,1)S(1)} %copy-done.26), kind=kOutput, calls=%fused_computation.10 | convolution fusion | flops 3023241216 | bytes 12189696 | tf_op jit(solution)/shard_map/dot_general | solution.py:304
  378.5 4.9 %collective-permute-start.25 = (bf16[384,2560]{1,0:T(8,128)(2,1)}, bf16[384,2560]{1,0:T(8,128)(2,1)}, u32[]{:S(2)}, u32[]{:S(2)}) collective-permute-start(bf16[384,2560]{1,0:T(8,128)(2,1)} %convolution_convert_fusion.2), channel_id=1, source_target_pairs={{0,1},{1,0},{2,3},{3,2},{4,5},{5,4},{6,7},{7,6},{8,9},{9,8},{10,11... | collective-permute-start | bytes 5898248 | tf_op jit(solution)/shard_map/ppermute | solution.py:308
  383.9 3.4 collective-permute-done.26
  387.5 20.5 %collective-permute-done.35 = bf16[640,1536]{1,0:T(8,128)(2,1)S(1)} collective-permute-done((bf16[640,1536]{1,0:T(8,128)(2,1)}, bf16[640,1536]{1,0:T(8,128)(2,1)S(1)}, u32[]{:S(2)}, u32[]{:S(2)}) %collective-permute-start.35) | collective-permute-done | bytes 1966112 | tf_op jit(solution)/shard_map/ppermute | solution.py:210
  410.5 4.7 collective-permute-start.38
  415.2 7.4 %fusion = bf16[384,2560]{1,0:T(8,128)(2,1)S(1)} fusion(bf16[2560,1536]{1,0:T(8,128)(2,1)} %constant_dynamic-update-slice_fusion.8, bf16[384,2560]{1,0:T(8,128)(2,1)} %collective-permute-done.25, bf16[768,768]{0,1:T(8,128)(2,1)} %copy-done.27, bf16[768,768]{0,1:T(8,128)(2,1)} %copy-done.25), kind=kOutput, calls=%fused_computation.11 | convolution fusion | flops 3025207296 | bytes 14155776 | tf_op jit(solution)/shard_map/dot_general | solution.py:304
  424.3 5.8 %collective-permute-start.30 = (bf16[48,2688]{1,0:T(8,128)(2,1)S(1)}, bf16[48,2688]{1,0:T(8,128)(2,1)S(1)}, u32[]{:S(2)}, u32[]{:S(2)}) collective-permute-start(bf16[48,2688]{1,0:T(8,128)(2,1)S(1)} %get-tuple-element.68), channel_id=1, source_target_pairs={{8,0},{10,2},{12,4},{14,6},{0,8},{2,10},{4,12},{6,14},{9,1},{11,3}... | collective-permute-start | bytes 774152 | tf_op jit(solution)/shard_map/ppermute | solution.py:317
  434.2 16.1 %collective-permute-start.39 = (bf16[160,1536]{1,0:T(8,128)(2,1)S(1)}, bf16[160,1536]{1,0:T(8,128)(2,1)S(1)}, u32[]{:S(2)}, u32[]{:S(2)}) collective-permute-start(bf16[160,1536]{1,0:T(8,128)(2,1)S(1)} %get-tuple-element.82), channel_id=1, source_target_pairs={{0,0},{8,1},{1,8},{9,9},{2,2},{10,3},{3,10},{11,11},{4,4},{12,5},{... | collective-permute-start | bytes 1474568 | tf_op jit(solution)/shard_map/ppermute | solution.py:322
  453.0 15.4 %collective-permute-done.31.refs_7_ = bf16[48,2688]{1,0:T(8,128)(2,1)S(1)} collective-permute-done((bf16[48,2688]{1,0:T(8,128)(2,1)S(1)}, bf16[48,2688]{1,0:T(8,128)(2,1)S(1)}, u32[]{:S(2)}, u32[]{:S(2)}) %collective-permute-start.31) | collective-permute-done | bytes 258080 | tf_op jit(solution)/shard_map/ppermute | solution.py:317
  468.4 5.5 %collective-permute-done.32.refs_8_ = bf16[48,2688]{1,0:T(8,128)(2,1)S(1)} collective-permute-done((bf16[48,2688]{1,0:T(8,128)(2,1)S(1)}, bf16[48,2688]{1,0:T(8,128)(2,1)S(1)}, u32[]{:S(2)}, u32[]{:S(2)}) %collective-permute-start.32) | collective-permute-done | bytes 258080 | tf_op jit(solution)/shard_map/ppermute | solution.py:317
  473.9 5.5 %collective-permute-done.33.refs_9_ = bf16[48,2688]{1,0:T(8,128)(2,1)S(1)} collective-permute-done((bf16[48,2688]{1,0:T(8,128)(2,1)S(1)}, bf16[48,2688]{1,0:T(8,128)(2,1)S(1)}, u32[]{:S(2)}, u32[]{:S(2)}) %collective-permute-start.33) | collective-permute-done | bytes 258080 | tf_op jit(solution)/shard_map/ppermute | solution.py:317
  (179 shorter events, 106.8 us)
Async XLA Ops:
  6.9 16.1 %collective-permute-start = (bf16[48,5248]{1,0:T(8,128)(2,1)}, bf16[48,5248]{1,0:T(8,128)(2,1)}, u32[]{:S(2)}, u32[]{:S(2)}) collective-permute-start(bf16[48,5248]{1,0:T(8,128)(2,1)} %get-tuple-element.22), channel_id=1, source_target_pairs={{0,2},{2,4},{4,6},{6,0},{8,10},{10,12},{12,14},{14,8},{1,3},{3,5},... | collective-permute-start | bytes 1511432 | tf_op jit(solution)/shard_map/ppermute | solution.py:270
  9.4 41.5 %collective-permute-start.1 = (bf16[48,5248]{1,0:T(8,128)(2,1)S(1)}, bf16[48,5248]{1,0:T(8,128)(2,1)}, u32[]{:S(2)}, u32[]{:S(2)}) collective-permute-start(bf16[48,5248]{1,0:T(8,128)(2,1)S(1)} %get-tuple-element.23), channel_id=1, source_target_pairs={{0,4},{2,6},{4,0},{6,2},{8,12},{10,14},{12,8},{14,10},{1,5},{3,7},... | collective-permute-start | bytes 1511432 | tf_op jit(solution)/shard_map/ppermute | solution.py:270
  12.7 40.1 %collective-permute-start.2 = (bf16[48,5248]{1,0:T(8,128)(2,1)S(1)}, bf16[48,5248]{1,0:T(8,128)(2,1)}, u32[]{:S(2)}, u32[]{:S(2)}) collective-permute-start(bf16[48,5248]{1,0:T(8,128)(2,1)S(1)} %get-tuple-element.24), channel_id=1, source_target_pairs={{0,6},{2,0},{4,2},{6,4},{8,14},{10,8},{12,10},{14,12},{1,7},{3,1},... | collective-permute-start | bytes 1511432 | tf_op jit(solution)/shard_map/ppermute | solution.py:270
  13.4 41.2 %collective-permute-start.3 = (bf16[48,5248]{1,0:T(8,128)(2,1)S(1)}, bf16[48,5248]{1,0:T(8,128)(2,1)}, u32[]{:S(2)}, u32[]{:S(2)}) collective-permute-start(bf16[48,5248]{1,0:T(8,128)(2,1)S(1)} %get-tuple-element.25), channel_id=1, source_target_pairs={{0,8},{2,10},{4,12},{6,14},{8,0},{10,2},{12,4},{14,6},{1,9},{3,11}... | collective-permute-start | bytes 1511432 | tf_op jit(solution)/shard_map/ppermute | solution.py:270
  14.7 41.7 %collective-permute-start.4 = (bf16[48,5248]{1,0:T(8,128)(2,1)S(1)}, bf16[48,5248]{1,0:T(8,128)(2,1)}, u32[]{:S(2)}, u32[]{:S(2)}) collective-permute-start(bf16[48,5248]{1,0:T(8,128)(2,1)S(1)} %get-tuple-element.26), channel_id=1, source_target_pairs={{0,10},{2,12},{4,14},{6,8},{8,2},{10,4},{12,6},{14,0},{1,11},{3,13... | collective-permute-start | bytes 1511432 | tf_op jit(solution)/shard_map/ppermute | solution.py:270
  23.0 35.3 %collective-permute-start.5 = (bf16[48,5248]{1,0:T(8,128)(2,1)S(1)}, bf16[48,5248]{1,0:T(8,128)(2,1)S(1)}, u32[]{:S(2)}, u32[]{:S(2)}) collective-permute-start(bf16[48,5248]{1,0:T(8,128)(2,1)S(1)} %get-tuple-element.27), channel_id=1, source_target_pairs={{0,12},{2,14},{4,8},{6,10},{8,4},{10,6},{12,0},{14,2},{1,13},{3,15... | collective-permute-start | bytes 1511432 | tf_op jit(solution)/shard_map/ppermute | solution.py:270
  50.8 14.5 %collective-permute-start.6 = (bf16[48,5248]{1,0:T(8,128)(2,1)S(1)}, bf16[48,5248]{1,0:T(8,128)(2,1)S(1)}, u32[]{:S(2)}, u32[]{:S(2)}) collective-permute-start(bf16[48,5248]{1,0:T(8,128)(2,1)S(1)} %get-tuple-element.28), channel_id=1, source_target_pairs={{0,14},{2,8},{4,10},{6,12},{8,6},{10,0},{12,2},{14,4},{1,15},{3,9}... | collective-permute-start | bytes 1511432 | tf_op jit(solution)/shard_map/ppermute | solution.py:270
  66.2 88.9 %collective-permute-start.7 = (bf16[384,5248]{1,0:T(8,128)(2,1)}, bf16[384,5248]{1,0:T(8,128)(2,1)}, u32[]{:S(2)}, u32[]{:S(2)}) collective-permute-start(bf16[384,5248]{1,0:T(8,128)(2,1)} %constant_dynamic-update-slice_fusion), channel_id=1, source_target_pairs={{0,1},{1,0},{2,3},{3,2},{4,5},{5,4},{6,7},{7,6},{8,9},{9,8},{10,11... | collective-permute-start | bytes 12091400 | tf_op jit(solution)/shard_map/ppermute | solution.py:273
  70.3 10.1 %collective-permute-start.14 = (bf16[160,1536]{1,0:T(8,128)(2,1)S(1)}, bf16[160,1536]{1,0:T(8,128)(2,1)S(1)}, u32[]{:S(2)}, u32[]{:S(2)}) collective-permute-start(bf16[160,1536]{1,0:T(8,128)(2,1)S(1)} %get-tuple-element.85), channel_id=1, source_target_pairs={{0,0},{1,8},{8,1},{9,9},{2,2},{3,10},{10,3},{11,11},{4,4},{5,12},{... | collective-permute-start | bytes 1474568 | tf_op jit(solution)/shard_map/ppermute | solution.py:257
  73.1 11.0 %collective-permute-start.15 = (bf16[160,1536]{1,0:T(8,128)(2,1)S(1)}, bf16[160,1536]{1,0:T(8,128)(2,1)S(1)}, u32[]{:S(2)}, u32[]{:S(2)}) collective-permute-start(bf16[160,1536]{1,0:T(8,128)(2,1)S(1)} %get-tuple-element.84), channel_id=1, source_target_pairs={{0,1},{1,9},{8,0},{9,8},{2,3},{3,11},{10,2},{11,10},{4,5},{5,13},{... | collective-permute-start | bytes 1474568 | tf_op jit(solution)/shard_map/ppermute | solution.py:258
  89.3 22.4 %collective-permute-start.16 = (bf16[320,1536]{1,0:T(8,128)(2,1)}, bf16[320,1536]{1,0:T(8,128)(2,1)S(1)}, u32[]{:S(2)}, u32[]{:S(2)}) collective-permute-start(bf16[320,1536]{1,0:T(8,128)(2,1)} %get-tuple-element.43), channel_id=1, source_target_pairs={{0,32},{32,64},{64,96},{96,0},{1,33},{33,65},{65,97},{97,1},{2,34}... | collective-permute-start | bytes 2949128 | tf_op jit(solution)/shard_map/ppermute | solution.py:156
  90.5 21.3 %collective-permute-start.17 = (bf16[320,1536]{1,0:T(8,128)(2,1)}, bf16[320,1536]{1,0:T(8,128)(2,1)S(1)}, u32[]{:S(2)}, u32[]{:S(2)}) collective-permute-start(bf16[320,1536]{1,0:T(8,128)(2,1)} %get-tuple-element.43), channel_id=1, source_target_pairs={{0,96},{32,0},{64,32},{96,64},{1,97},{33,1},{65,33},{97,65},{2,98}... | collective-permute-start | bytes 2949128 | tf_op jit(solution)/shard_map/ppermute | solution.py:157
  92.0 22.6 %collective-permute-start.20 = (bf16[320,1536]{1,0:T(8,128)(2,1)}, bf16[320,1536]{1,0:T(8,128)(2,1)S(1)}, u32[]{:S(2)}, u32[]{:S(2)}) collective-permute-start(bf16[320,1536]{1,0:T(8,128)(2,1)} %get-tuple-element.43), channel_id=1, source_target_pairs={{0,16},{16,0},{1,17},{17,1},{2,18},{18,2},{3,19},{19,3},{4,20},{20... | collective-permute-start | bytes 2949128 | tf_op jit(solution)/shard_map/ppermute | solution.py:165
  98.0 70.7 %copy-start.11 = (bf16[384,2560]{1,0:T(8,128)(2,1)}, bf16[384,2560]{1,0:T(8,128)(2,1)S(1)}, u32[]{:S(2)}) copy-start(bf16[384,2560]{1,0:T(8,128)(2,1)S(1)} %get-tuple-element.53) | copy-start | bytes 5898244
  111.7 10.8 %collective-permute-start.18 = (bf16[160,1536]{1,0:T(8,128)(2,1)S(1)}, bf16[160,1536]{1,0:T(8,128)(2,1)S(1)}, u32[]{:S(2)}, u32[]{:S(2)}) collective-permute-start(bf16[160,1536]{1,0:T(8,128)(2,1)S(1)} %slice.190), channel_id=1, source_target_pairs={{0,32},{32,64},{64,96},{96,0},{1,33},{33,65},{65,97},{97,1},{2,34}... | collective-permute-start | bytes 1474568 | tf_op jit(solution)/shard_map/ppermute | solution.py:158
  111.9 11.5 %collective-permute-start.19 = (bf16[160,1536]{1,0:T(8,128)(2,1)S(1)}, bf16[160,1536]{1,0:T(8,128)(2,1)S(1)}, u32[]{:S(2)}, u32[]{:S(2)}) collective-permute-start(bf16[160,1536]{1,0:T(8,128)(2,1)S(1)} %slice.191), channel_id=1, source_target_pairs={{0,96},{32,0},{64,32},{96,64},{1,97},{33,1},{65,33},{97,65},{2,98}... | collective-permute-start | bytes 1474568 | tf_op jit(solution)/shard_map/ppermute | solution.py:159
  114.6 29.0 %collective-permute-start.21 = (bf16[320,1536]{1,0:T(8,128)(2,1)S(1)}, bf16[320,1536]{1,0:T(8,128)(2,1)S(1)}, u32[]{:S(2)}, u32[]{:S(2)}) collective-permute-start(bf16[320,1536]{1,0:T(8,128)(2,1)S(1)} %collective-permute-done.20), channel_id=1, source_target_pairs={{0,32},{32,64},{64,96},{96,0},{1,33},{33,65},{65,97},{97,1},{2,34}... | collective-permute-start | bytes 2949128 | tf_op jit(solution)/shard_map/ppermute | solution.py:156
  114.6 29.1 %collective-permute-start.22 = (bf16[320,1536]{1,0:T(8,128)(2,1)S(1)}, bf16[320,1536]{1,0:T(8,128)(2,1)S(1)}, u32[]{:S(2)}, u32[]{:S(2)}) collective-permute-start(bf16[320,1536]{1,0:T(8,128)(2,1)S(1)} %collective-permute-done.20), channel_id=1, source_target_pairs={{0,96},{32,0},{64,32},{96,64},{1,97},{33,1},{65,33},{97,65},{2,98}... | collective-permute-start | bytes 2949128 | tf_op jit(solution)/shard_map/ppermute | solution.py:157
  143.6 9.9 %collective-permute-start.23 = (bf16[160,1536]{1,0:T(8,128)(2,1)S(1)}, bf16[160,1536]{1,0:T(8,128)(2,1)S(1)}, u32[]{:S(2)}, u32[]{:S(2)}) collective-permute-start(bf16[160,1536]{1,0:T(8,128)(2,1)S(1)} %slice.192), channel_id=1, source_target_pairs={{0,32},{32,64},{64,96},{96,0},{1,33},{33,65},{65,97},{97,1},{2,34}... | collective-permute-start | bytes 1474568 | tf_op jit(solution)/shard_map/ppermute | solution.py:158
  143.8 10.5 %collective-permute-start.24 = (bf16[160,1536]{1,0:T(8,128)(2,1)S(1)}, bf16[160,1536]{1,0:T(8,128)(2,1)S(1)}, u32[]{:S(2)}, u32[]{:S(2)}) collective-permute-start(bf16[160,1536]{1,0:T(8,128)(2,1)S(1)} %slice.193), channel_id=1, source_target_pairs={{0,96},{32,0},{64,32},{96,64},{1,97},{33,1},{65,33},{97,65},{2,98}... | collective-permute-start | bytes 1474568 | tf_op jit(solution)/shard_map/ppermute | solution.py:159
  174.1 9.0 %collective-permute-start.41 = (bf16[96,2560]{1,0:T(8,128)(2,1)S(1)}, bf16[96,2560]{1,0:T(8,128)(2,1)S(1)}, u32[]{:S(2)}, u32[]{:S(2)}) collective-permute-start(bf16[96,2560]{1,0:T(8,128)(2,1)S(1)} %get-tuple-element.59), channel_id=1, source_target_pairs={{0,32},{32,64},{64,96},{96,0},{1,33},{33,65},{65,97},{97,1},{2,34}... | collective-permute-start | bytes 1474568 | tf_op jit(solution)/shard_map/ppermute | solution.py:206
  174.2 8.9 %collective-permute-start.43 = (bf16[96,2560]{1,0:T(8,128)(2,1)S(1)}, bf16[96,2560]{1,0:T(8,128)(2,1)S(1)}, u32[]{:S(2)}, u32[]{:S(2)}) collective-permute-start(bf16[96,2560]{1,0:T(8,128)(2,1)S(1)} %get-tuple-element.60), channel_id=1, source_target_pairs={{0,96},{32,0},{64,32},{96,64},{1,97},{33,1},{65,33},{97,65},{2,98}... | collective-permute-start | bytes 1474568 | tf_op jit(solution)/shard_map/ppermute | solution.py:207
  185.5 18.6 %collective-permute-start.42 = (bf16[192,2560]{1,0:T(8,128)(2,1)}, bf16[192,2560]{1,0:T(8,128)(2,1)}, u32[]{:S(2)}, u32[]{:S(2)}) collective-permute-start(bf16[192,2560]{1,0:T(8,128)(2,1)} %pad_maximum_fusion.12), channel_id=1, source_target_pairs={{0,32},{32,64},{64,96},{96,0},{1,33},{33,65},{65,97},{97,1},{2,34}... | collective-permute-start | bytes 2949128 | tf_op jit(solution)/shard_map/ppermute | solution.py:210
  186.9 17.2 %collective-permute-start.44 = (bf16[192,2560]{1,0:T(8,128)(2,1)}, bf16[192,2560]{1,0:T(8,128)(2,1)}, u32[]{:S(2)}, u32[]{:S(2)}) collective-permute-start(bf16[192,2560]{1,0:T(8,128)(2,1)} %pad_maximum_fusion.13), channel_id=1, source_target_pairs={{0,96},{32,0},{64,32},{96,64},{1,97},{33,1},{65,33},{97,65},{2,98}... | collective-permute-start | bytes 2949128 | tf_op jit(solution)/shard_map/ppermute | solution.py:211
  206.4 9.4 %collective-permute-start.45 = (bf16[96,2560]{1,0:T(8,128)(2,1)}, bf16[96,2560]{1,0:T(8,128)(2,1)S(1)}, u32[]{:S(2)}, u32[]{:S(2)}) collective-permute-start(bf16[96,2560]{1,0:T(8,128)(2,1)} %add_convert_fusion.6), channel_id=1, source_target_pairs={{0,16},{16,0},{1,17},{17,1},{2,18},{18,2},{3,19},{19,3},{4,20},{20... | collective-permute-start | bytes 1474568 | tf_op jit(solution)/shard_map/ppermute | solution.py:217
  217.4 30.2 %collective-permute-start.46 = (bf16[96,2560]{1,0:T(8,128)(2,1)S(1)}, bf16[96,2560]{1,0:T(8,128)(2,1)S(1)}, u32[]{:S(2)}, u32[]{:S(2)}) collective-permute-start(bf16[96,2560]{1,0:T(8,128)(2,1)S(1)} %add_convert_fusion.5), channel_id=1, source_target_pairs={{0,0},{8,1},{16,8},{24,9},{32,16},{40,17},{48,24},{56,25},{1,32},{... | collective-permute-start | bytes 1474568 | tf_op jit(solution)/shard_map/ppermute | solution.py:332
  249.8 18.3 %collective-permute-start.8 = (bf16[96,2560]{1,0:T(8,128)(2,1)S(1)}, bf16[96,2560]{1,0:T(8,128)(2,1)S(1)}, u32[]{:S(2)}, u32[]{:S(2)}) collective-permute-start(bf16[96,2560]{1,0:T(8,128)(2,1)S(1)} %get-tuple-element.71), channel_id=1, source_target_pairs={{0,0},{1,8},{8,16},{9,24},{16,32},{17,40},{24,48},{25,56},{32,1},{... | collective-permute-start | bytes 1474568 | tf_op jit(solution)/shard_map/ppermute | solution.py:262
  268.1 13.2 %collective-permute-start.9 = (bf16[96,2560]{1,0:T(8,128)(2,1)S(1)}, bf16[96,2560]{1,0:T(8,128)(2,1)S(1)}, u32[]{:S(2)}, u32[]{:S(2)}) collective-permute-start(bf16[96,2560]{1,0:T(8,128)(2,1)S(1)} %collective-permute-done.8), channel_id=1, source_target_pairs={{0,16},{16,0},{1,17},{17,1},{2,18},{18,2},{3,19},{19,3},{4,20},{20... | collective-permute-start | bytes 1474568 | tf_op jit(solution)/shard_map/ppermute | solution.py:183
  284.6 22.6 %collective-permute-start.10 = (bf16[192,2560]{1,0:T(8,128)(2,1)S(1)}, bf16[192,2560]{1,0:T(8,128)(2,1)S(1)}, u32[]{:S(2)}, u32[]{:S(2)}) collective-permute-start(bf16[192,2560]{1,0:T(8,128)(2,1)S(1)} %get-tuple-element.41), channel_id=1, source_target_pairs={{0,32},{32,64},{64,96},{96,0},{1,33},{33,65},{65,97},{97,1},{2,34}... | collective-permute-start | bytes 2949128 | tf_op jit(solution)/shard_map/ppermute | solution.py:156
  284.6 24.0 %collective-permute-start.11 = (bf16[192,2560]{1,0:T(8,128)(2,1)S(1)}, bf16[192,2560]{1,0:T(8,128)(2,1)S(1)}, u32[]{:S(2)}, u32[]{:S(2)}) collective-permute-start(bf16[192,2560]{1,0:T(8,128)(2,1)S(1)} %get-tuple-element.41), channel_id=1, source_target_pairs={{0,96},{32,0},{64,32},{96,64},{1,97},{33,1},{65,33},{97,65},{2,98}... | collective-permute-start | bytes 2949128 | tf_op jit(solution)/shard_map/ppermute | solution.py:157
  307.2 11.4 %collective-permute-start.12 = (bf16[96,2560]{1,0:T(8,128)(2,1)S(1)}, bf16[96,2560]{1,0:T(8,128)(2,1)S(1)}, u32[]{:S(2)}, u32[]{:S(2)}) collective-permute-start(bf16[96,2560]{1,0:T(8,128)(2,1)S(1)} %slice.178), channel_id=1, source_target_pairs={{0,32},{32,64},{64,96},{96,0},{1,33},{33,65},{65,97},{97,1},{2,34}... | collective-permute-start | bytes 1474568 | tf_op jit(solution)/shard_map/ppermute | solution.py:158
  308.6 11.1 %collective-permute-start.13 = (bf16[96,2560]{1,0:T(8,128)(2,1)S(1)}, bf16[96,2560]{1,0:T(8,128)(2,1)S(1)}, u32[]{:S(2)}, u32[]{:S(2)}) collective-permute-start(bf16[96,2560]{1,0:T(8,128)(2,1)S(1)} %slice.179), channel_id=1, source_target_pairs={{0,96},{32,0},{64,32},{96,64},{1,97},{33,1},{65,33},{97,65},{2,98}... | collective-permute-start | bytes 1474568 | tf_op jit(solution)/shard_map/ppermute | solution.py:159
  340.4 21.2 %collective-permute-start.34 = (bf16[320,1536]{1,0:T(8,128)(2,1)}, bf16[320,1536]{1,0:T(8,128)(2,1)S(1)}, u32[]{:S(2)}, u32[]{:S(2)}) collective-permute-start(bf16[320,1536]{1,0:T(8,128)(2,1)} %get-tuple-element.46), channel_id=1, source_target_pairs={{0,32},{32,64},{64,96},{96,0},{1,33},{33,65},{65,97},{97,1},{2,34}... | collective-permute-start | bytes 2949128 | tf_op jit(solution)/shard_map/ppermute | solution.py:206
  341.6 21.0 %collective-permute-start.36 = (bf16[320,1536]{1,0:T(8,128)(2,1)}, bf16[320,1536]{1,0:T(8,128)(2,1)}, u32[]{:S(2)}, u32[]{:S(2)}) collective-permute-start(bf16[320,1536]{1,0:T(8,128)(2,1)} %get-tuple-element.47), channel_id=1, source_target_pairs={{0,96},{32,0},{64,32},{96,64},{1,97},{33,1},{65,33},{97,65},{2,98}... | collective-permute-start | bytes 2949128 | tf_op jit(solution)/shard_map/ppermute | solution.py:207
  366.6 41.4 %collective-permute-start.35 = (bf16[640,1536]{1,0:T(8,128)(2,1)}, bf16[640,1536]{1,0:T(8,128)(2,1)S(1)}, u32[]{:S(2)}, u32[]{:S(2)}) collective-permute-start(bf16[640,1536]{1,0:T(8,128)(2,1)} %pad_maximum_fusion.8), channel_id=1, source_target_pairs={{0,32},{32,64},{64,96},{96,0},{1,33},{33,65},{65,97},{97,1},{2,34}... | collective-permute-start | bytes 5898248 | tf_op jit(solution)/shard_map/ppermute | solution.py:210
  368.3 40.2 %collective-permute-start.37 = (bf16[640,1536]{1,0:T(8,128)(2,1)}, bf16[640,1536]{1,0:T(8,128)(2,1)}, u32[]{:S(2)}, u32[]{:S(2)}) collective-permute-start(bf16[640,1536]{1,0:T(8,128)(2,1)} %pad_maximum_fusion.9), channel_id=1, source_target_pairs={{0,96},{32,0},{64,32},{96,64},{1,97},{33,1},{65,33},{97,65},{2,98}... | collective-permute-start | bytes 5898248 | tf_op jit(solution)/shard_map/ppermute | solution.py:211
  378.5 36.7 %collective-permute-start.25 = (bf16[384,2560]{1,0:T(8,128)(2,1)}, bf16[384,2560]{1,0:T(8,128)(2,1)}, u32[]{:S(2)}, u32[]{:S(2)}) collective-permute-start(bf16[384,2560]{1,0:T(8,128)(2,1)} %convolution_convert_fusion.2), channel_id=1, source_target_pairs={{0,1},{1,0},{2,3},{3,2},{4,5},{5,4},{6,7},{7,6},{8,9},{9,8},{10,11... | collective-permute-start | bytes 5898248 | tf_op jit(solution)/shard_map/ppermute | solution.py:308
  383.6 3.8 collective-permute-start.26
  410.5 21.6 %collective-permute-start.38 = (bf16[320,1536]{1,0:T(8,128)(2,1)S(1)}, bf16[320,1536]{1,0:T(8,128)(2,1)S(1)}, u32[]{:S(2)}, u32[]{:S(2)}) collective-permute-start(bf16[320,1536]{1,0:T(8,128)(2,1)S(1)} %add_convert_fusion.1), channel_id=1, source_target_pairs={{0,16},{16,0},{1,17},{17,1},{2,18},{18,2},{3,19},{19,3},{4,20},{20... | collective-permute-start | bytes 2949128 | tf_op jit(solution)/shard_map/ppermute | solution.py:217
  422.8 27.6 %collective-permute-start.27 = (bf16[48,2688]{1,0:T(8,128)(2,1)S(1)}, bf16[48,2688]{1,0:T(8,128)(2,1)S(1)}, u32[]{:S(2)}, u32[]{:S(2)}) collective-permute-start(bf16[48,2688]{1,0:T(8,128)(2,1)S(1)} %get-tuple-element.65), channel_id=1, source_target_pairs={{2,0},{4,2},{6,4},{0,6},{10,8},{12,10},{14,12},{8,14},{3,1},{5,3},... | collective-permute-start | bytes 774152 | tf_op jit(solution)/shard_map/ppermute | solution.py:317
  422.9 27.6 %collective-permute-start.28 = (bf16[48,2688]{1,0:T(8,128)(2,1)S(1)}, bf16[48,2688]{1,0:T(8,128)(2,1)S(1)}, u32[]{:S(2)}, u32[]{:S(2)}) collective-permute-start(bf16[48,2688]{1,0:T(8,128)(2,1)S(1)} %get-tuple-element.66), channel_id=1, source_target_pairs={{4,0},{6,2},{0,4},{2,6},{12,8},{14,10},{8,12},{10,14},{5,1},{7,3},... | collective-permute-start | bytes 774152 | tf_op jit(solution)/shard_map/ppermute | solution.py:317
  423.0 27.6 %collective-permute-start.29 = (bf16[48,2688]{1,0:T(8,128)(2,1)S(1)}, bf16[48,2688]{1,0:T(8,128)(2,1)S(1)}, u32[]{:S(2)}, u32[]{:S(2)}) collective-permute-start(bf16[48,2688]{1,0:T(8,128)(2,1)S(1)} %get-tuple-element.67), channel_id=1, source_target_pairs={{6,0},{0,2},{2,4},{4,6},{14,8},{8,10},{10,12},{12,14},{7,1},{1,3},... | collective-permute-start | bytes 774152 | tf_op jit(solution)/shard_map/ppermute | solution.py:317
  424.3 26.3 %collective-permute-start.30 = (bf16[48,2688]{1,0:T(8,128)(2,1)S(1)}, bf16[48,2688]{1,0:T(8,128)(2,1)S(1)}, u32[]{:S(2)}, u32[]{:S(2)}) collective-permute-start(bf16[48,2688]{1,0:T(8,128)(2,1)S(1)} %get-tuple-element.68), channel_id=1, source_target_pairs={{8,0},{10,2},{12,4},{14,6},{0,8},{2,10},{4,12},{6,14},{9,1},{11,3}... | collective-permute-start | bytes 774152 | tf_op jit(solution)/shard_map/ppermute | solution.py:317
  434.2 47.4 %collective-permute-start.39 = (bf16[160,1536]{1,0:T(8,128)(2,1)S(1)}, bf16[160,1536]{1,0:T(8,128)(2,1)S(1)}, u32[]{:S(2)}, u32[]{:S(2)}) collective-permute-start(bf16[160,1536]{1,0:T(8,128)(2,1)S(1)} %get-tuple-element.82), channel_id=1, source_target_pairs={{0,0},{8,1},{1,8},{9,9},{2,2},{10,3},{3,10},{11,11},{4,4},{12,5},{... | collective-permute-start | bytes 1474568 | tf_op jit(solution)/shard_map/ppermute | solution.py:322
  450.4 31.2 %collective-permute-start.40 = (bf16[160,1536]{1,0:T(8,128)(2,1)S(1)}, bf16[160,1536]{1,0:T(8,128)(2,1)S(1)}, u32[]{:S(2)}, u32[]{:S(2)}) collective-permute-start(bf16[160,1536]{1,0:T(8,128)(2,1)S(1)} %get-tuple-element.83), channel_id=1, source_target_pairs={{1,0},{9,1},{0,8},{8,9},{3,2},{11,3},{2,10},{10,11},{5,4},{13,5},{... | collective-permute-start | bytes 1474568 | tf_op jit(solution)/shard_map/ppermute | solution.py:327
  450.5 17.9 %collective-permute-start.31 = (bf16[48,2688]{1,0:T(8,128)(2,1)S(1)}, bf16[48,2688]{1,0:T(8,128)(2,1)S(1)}, u32[]{:S(2)}, u32[]{:S(2)}) collective-permute-start(bf16[48,2688]{1,0:T(8,128)(2,1)S(1)} %get-tuple-element.69), channel_id=1, source_target_pairs={{10,0},{12,2},{14,4},{8,6},{2,8},{4,10},{6,12},{0,14},{11,1},{13,3... | collective-permute-start | bytes 774152 | tf_op jit(solution)/shard_map/ppermute | solution.py:317
  450.6 23.4 %collective-permute-start.32 = (bf16[48,2688]{1,0:T(8,128)(2,1)S(1)}, bf16[48,2688]{1,0:T(8,128)(2,1)S(1)}, u32[]{:S(2)}, u32[]{:S(2)}) collective-permute-start(bf16[48,2688]{1,0:T(8,128)(2,1)S(1)} %get-tuple-element.70), channel_id=1, source_target_pairs={{12,0},{14,2},{8,4},{10,6},{4,8},{6,10},{0,12},{2,14},{13,1},{15,3... | collective-permute-start | bytes 774152 | tf_op jit(solution)/shard_map/ppermute | solution.py:317
  450.7 28.8 %collective-permute-start.33 = (bf16[48,2688]{1,0:T(8,128)(2,1)S(1)}, bf16[48,2688]{1,0:T(8,128)(2,1)S(1)}, u32[]{:S(2)}, u32[]{:S(2)}) collective-permute-start(bf16[48,2688]{1,0:T(8,128)(2,1)S(1)} %get-tuple-element.63), channel_id=1, source_target_pairs={{14,0},{8,2},{10,4},{12,6},{6,8},{0,10},{2,12},{4,14},{15,1},{9,3}... | collective-permute-start | bytes 774152 | tf_op jit(solution)/shard_map/ppermute | solution.py:317
  (29 other events, 414.3 us)

commit v3 on v2

v3 whole, which is shorter than its diff:
```python
import jax
import jax.numpy as jnp
from jax import lax
from jax.experimental import pallas as pl
from jax.experimental.pallas import tpu as pltpu
from jax.sharding import Mesh
from jax.sharding import PartitionSpec as P

beta_one = 0.9
beta_two = 0.95
learn_rate = 0.003
decay_rate = 0.1
epsilon = 1e-08
correct_one = 1.0 - 2.6561398887587e-05
correct_two = 1.0 - 0.005920529220333

LANES = 128
GROUPS = 8
f32 = jnp.float32
bf16 = jnp.bfloat16

PLUS = [(i, (i + 1) % 4) for i in range(4)]
MINUS = [(i, (i - 1) % 4) for i in range(4)]
SWAP = [(0, 1), (1, 0)]
PAIR_A = [(2 * yl + c, 2 * c + yl) for yl in range(2) for c in range(2)]
PAIR_B = [(2 * yl + c, 2 * c + 1 - yl) for yl in range(2) for c in range(2)]


def _cycle():
    pairs = []
    for x1 in range(2):
        for x0 in range(2):
            for yh in range(2):
                for yl in range(2):
                    for c in range(2):
                        src = (((x1 * 2 + x0) * 2 + yh) * 2 + yl) * 2 + c
                        dst = (((x1 * 2 + yh) * 2 + yl) * 2 + c) * 2 + x0
                        pairs.append((src, dst))
    return pairs


CYCLE = _cycle()
CYCLE_AXES = ("x", "yh", "yl", "c")


def back(pairs):
    return [(d, s) for s, d in pairs]


def after(value, *earlier):
    return lax.optimization_barrier((value, earlier))[0]


def adamw(weight, moment, second, grad):
    moment_new = beta_one * moment + (1.0 - beta_one) * grad
    second_new = beta_two * second + (1.0 - beta_two) * grad * grad
    update = moment_new / correct_one / (jnp.sqrt(second_new / correct_two) + epsilon)
    return (weight - learn_rate * (update + decay_rate * weight), moment_new, second_new)


def one_hots(ids, capacity):
    tok = ids.shape[1]
    experts = lax.broadcasted_iota(jnp.int32, (GROUPS, tok), 0)
    named = [(experts == ids[k : k + 1, :]).astype(f32) for k in range(2)]
    earlier = (
        lax.broadcasted_iota(jnp.int32, (tok, tok), 0)
        < lax.broadcasted_iota(jnp.int32, (tok, tok), 1)
    ).astype(f32)
    count = jnp.dot(
        (named[0] + named[1]).astype(bf16), earlier.astype(bf16), preferred_element_type=f32
    )
    slot = lax.broadcasted_iota(jnp.int32, (GROUPS * capacity, tok), 0)
    hots = []
    for k in range(2):
        rank = jnp.sum(named[k] * count, axis=0, keepdims=True).astype(jnp.int32)
        expert = ids[k : k + 1, :]
        dest = ((expert & 1) * 4 + (expert >> 1)) * capacity + rank
        hots.append((slot == dest).astype(f32))
    return hots


def block_of(width):
    return 512 if width % 512 == 0 else width


def pack_kernel(capacity, width, ids_ref, probs_ref, x_ref, y_ref, out_ref):
    first, second = one_hots(ids_ref[...], capacity)
    hot = (first + second).astype(bf16)
    probs = probs_ref[...]
    gates = (first * probs[0:1, :] + second * probs[1:2, :]).astype(bf16)
    ones = jnp.ones((gates.shape[1], LANES), bf16)
    out_ref[:, 2 * width :] = jnp.dot(gates, ones, preferred_element_type=f32).astype(bf16)
    block = block_of(width)

    def step(i, carry):
        at = pl.multiple_of(i * block, block)
        cols = pl.ds(at, block)
        out_ref[:, cols] = jnp.dot(
            hot, x_ref[:, cols], preferred_element_type=f32
        ).astype(bf16)
        out_ref[:, pl.ds(pl.multiple_of(at + width, block), block)] = jnp.dot(
            hot, y_ref[:, cols], preferred_element_type=f32
        ).astype(bf16)
        return carry

    lax.fori_loop(0, width // block, step, 0)


def unpack_kernel(capacity, width, ids_ref, rows_ref, x_ref, prob_ref):
    first, second = one_hots(ids_ref[...], capacity)
    hot = (first + second).astype(bf16)
    block = block_of(width)

    def step(i, carry):
        cols = pl.ds(pl.multiple_of(i * block, block), block)
        x_ref[:, cols] = lax.dot_general(
            hot, rows_ref[:, cols], (((0,), (0,)), ((), ())), preferred_element_type=f32
        ).astype(bf16)
        return carry

    lax.fori_loop(0, width // block, step, 0)
    q_col = rows_ref[:, width:].astype(f32)
    prob_ref[0:1, :] = jnp.sum(first * q_col, axis=0, keepdims=True).astype(bf16)
    prob_ref[1:2, :] = jnp.sum(second * q_col, axis=0, keepdims=True).astype(bf16)


def vmem_specs(count):
    return [pl.BlockSpec(memory_space=pltpu.VMEM) for _ in range(count)]


def pack_rows(ids, probs, x, y, capacity):
    width = x.shape[1]
    return pl.pallas_call(
        lambda *refs: pack_kernel(capacity, width, *refs),
        out_shape=jax.ShapeDtypeStruct((GROUPS * capacity, 2 * width + LANES), bf16),
        in_specs=vmem_specs(4),
        out_specs=vmem_specs(1)[0],
        compiler_params=pltpu.CompilerParams(vmem_limit_bytes=40 << 20),
        name="pack_rows",
    )(ids, probs, x, y)


def unpack_rows(ids, rows, width, capacity):
    tok = ids.shape[1]
    return pl.pallas_call(
        lambda *refs: unpack_kernel(capacity, width, *refs),
        out_shape=(
            jax.ShapeDtypeStruct((tok, width), bf16),
            jax.ShapeDtypeStruct((2, tok), bf16),
        ),
        in_specs=vmem_specs(2),
        out_specs=tuple(vmem_specs(2)),
        compiler_params=pltpu.CompilerParams(vmem_limit_bytes=40 << 20),
        name="unpack_rows",
    )(ids, rows)


def put(whole, part, row):
    return lax.dynamic_update_slice(whole, part, (row, 0))


def neighbours(part):
    return lax.ppermute(part, "x", PLUS), lax.ppermute(part, "x", MINUS)


def far(left, right, half):
    return lax.ppermute(left[:half], "x", PLUS), lax.ppermute(right[half:], "x", MINUS)


def place_all(size, rows_of, sets):
    whole = jnp.zeros((8 * size, sets[0][0].shape[1]), bf16)
    for index, (part, left, right, top, low) in enumerate(sets):
        whole = put(whole, part, rows_of(0, index))
        whole = put(whole, left, rows_of(3, index))
        whole = put(whole, right, rows_of(1, index))
        whole = put(whole, top, rows_of(2, index))
        whole = put(whole, low, rows_of(2, index) + top.shape[0])
    return whole


def plus(*values):
    return sum(v.astype(f32) for v in values).astype(bf16)


class Scatter:
    def __init__(self, terms, x, yh):
        self.terms, self.x, self.yh = terms, x, yh
        self.size, self.n = terms.shape[0] // 8, terms.shape[1]

    def rows(self, k, side, count):
        start = self.size * (2 * ((self.x + k) % 4) + side)
        return lax.dynamic_slice(self.terms, (start, 0), (count * self.size, self.n))

    def first(self, *earlier):
        top, low = after((self.rows(2, 0, 1), self.rows(2, 1, 1)), *earlier)
        self.got = lax.ppermute(top, "x", PLUS), lax.ppermute(low, "x", MINUS)
        return self.got

    def second(self, *earlier):
        from_left, from_right = self.got
        to_right = jnp.concatenate((plus(self.rows(1, 0, 1), from_left), self.rows(1, 1, 1)))
        to_left = jnp.concatenate((self.rows(3, 0, 1), plus(self.rows(3, 1, 1), from_right)))
        to_right, to_left = after((to_right, to_left), *earlier)
        self.got = lax.ppermute(to_right, "x", PLUS), lax.ppermute(to_left, "x", MINUS)
        return self.got

    def last(self, *earlier):
        def mine(side):
            cut = lambda v: lax.dynamic_slice(v, (self.size * side, 0), (self.size, self.n))
            return plus(self.rows(0, side, 1), *(cut(v) for v in self.got))

        sent = lax.ppermute(after(mine(1 - self.yh), *earlier), "yh", SWAP)
        return plus(mine(self.yh), sent)


def body(
    layer_input,
    output_grad,
    expert_ids,
    gate_probs,
    gate_weight,
    up_weight,
    down_weight,
    gate_moment,
    up_moment,
    down_moment,
    gate_second,
    up_second,
    down_second,
):
    x, yh, yl = lax.axis_index("x"), lax.axis_index("yh"), lax.axis_index("yl")
    z, c = lax.axis_index("z"), lax.axis_index("c")
    tok, picks = expert_ids.shape
    capacity = 3 * tok * picks // (2 * GROUPS)
    width = layer_input.shape[1]
    hidden_units = gate_weight.shape[2]
    quarter = hidden_units // 4
    half = hidden_units // 2
    rows = GROUPS * capacity
    depth = gate_weight.shape[1]

    gate_low, up_low = gate_weight[0].astype(bf16), up_weight[0].astype(bf16)

    def chunk(core):
        cuts = [
            w[:, (core + 2 * k) * quarter : (core + 2 * k + 1) * quarter]
            for w in (gate_low, up_low)
            for k in range(2)
        ]
        return jnp.concatenate(cuts, axis=1)

    chunks = (chunk(0), chunk(1))
    part_a = lax.ppermute(jnp.where(yl == 0, chunks[0], chunks[1]), ("yl", "c"), PAIR_A)
    part_b = lax.ppermute(jnp.where(yl == 0, chunks[1], chunks[0]), ("yl", "c"), PAIR_B)
    part = jnp.where(
        c == 0, jnp.concatenate((part_a, part_b)), jnp.concatenate((part_b, part_a))
    )
    down_part = lax.ppermute(down_weight[0].astype(bf16), CYCLE_AXES, CYCLE)

    ids = expert_ids.T
    sent = pack_rows(ids, gate_probs.T.astype(f32), layer_input, output_grad, capacity)
    own = lax.all_to_all(
        sent.reshape(GROUPS, capacity, -1), ("yl", "z"), 0, 0, tiled=True
    ).reshape(rows, -1)

    part_other = lax.ppermute(part, "yh", SWAP)
    down_other = lax.ppermute(down_part, "yh", SWAP)
    near_own = neighbours(part)
    near_other = neighbours(after(part_other, *near_own))
    far_own = far(*near_own, depth)
    far_other = far(*near_other, depth)
    size_down = down_part.shape[0]
    both = jnp.where(
        yh == 0,
        jnp.concatenate((down_part, down_other)),
        jnp.concatenate((down_other, down_part)),
    )
    both = after(both, *near_other, *far_own)
    near_down = neighbours(both)
    far_down = far(*near_down, size_down)
    w_gate_up = place_all(
        2 * depth,
        lambda k, index: 2 * depth * (2 * ((x + k) % 4) + (1 - yh if index else yh)),
        ((part, *near_own, *far_own), (part_other, *near_other, *far_other)),
    )
    w_down = place_all(
        size_down,
        lambda k, index: 2 * size_down * ((x + k) % 4),
        ((both, *near_down, *far_down),),
    )
    other = lax.ppermute(own, "c", SWAP)
    x_rows = jnp.concatenate((own[:, :width], other[:, :width]))
    y_rows = jnp.concatenate((own[:, width : 2 * width], other[:, width : 2 * width]))
    gates = jnp.concatenate((own[:, 2 * width :], other[:, 2 * width :]))[:, :1].astype(f32)

    pre = jnp.dot(x_rows, w_gate_up, preferred_element_type=f32)
    gate_pre, up_pre = pre[:, :half], pre[:, half:]
    sigmoid_gate = jax.nn.sigmoid(gate_pre)
    silu_gate = gate_pre * sigmoid_gate
    hidden_full = silu_gate * up_pre
    hidden = hidden_full.astype(bf16)
    hidden_scaled = (gates * hidden_full).astype(bf16)
    down_term = lax.dot_general(
        hidden_scaled, y_rows, (((0,), (0,)), ((), ())), preferred_element_type=f32
    ).astype(bf16)
    down_sum = Scatter(down_term, x, yh)
    down_sum.first(*near_down)
    down_second_got = down_sum.second(*far_down)
    raw_grad = lax.dot_general(
        y_rows, w_down, (((1,), (1,)), ((), ())), preferred_element_type=f32
    )
    prob_rows = jnp.sum(hidden.astype(f32) * raw_grad, axis=1, keepdims=True)
    hidden_grad = gates * raw_grad
    dsilu = sigmoid_gate * (1.0 + gate_pre * (1.0 - sigmoid_gate))
    pre_grad = jnp.concatenate(
        (hidden_grad * up_pre * dsilu, hidden_grad * silu_gate), axis=1
    ).astype(bf16)
    gate_up_term = lax.dot_general(
        x_rows, pre_grad, (((0,), (0,)), ((), ())), preferred_element_type=f32
    ).astype(bf16)
    gate_up_sum = Scatter(gate_up_term, x, yh)
    gate_up_first = gate_up_sum.first(*down_second_got)
    grad_down = down_sum.last(gate_up_term)
    gate_up_sum.second()
    pre_grad = after(pre_grad, gate_up_term)

    def input_part(d_rows):
        return lax.dot_general(
            d_rows, w_gate_up, (((1,), (1,)), ((), ())), preferred_element_type=f32
        )

    far_rows = lax.ppermute(input_part(pre_grad[rows:]).astype(bf16), "c", SWAP)
    far_prob = lax.ppermute(
        jnp.broadcast_to(prob_rows[rows:], (rows, LANES)), "c", SWAP
    )
    near_rows = (input_part(pre_grad[:rows]) + far_rows.astype(f32)).astype(bf16)
    near_prob = (prob_rows[:rows] + far_prob).astype(bf16)
    packed = jnp.concatenate((near_rows, near_prob), axis=1)
    returned = lax.all_to_all(
        packed.reshape(GROUPS, capacity, -1), ("yl", "z"), 0, 0, tiled=True
    ).reshape(rows, -1)
    input_grad, prob_grad = unpack_rows(ids, returned, width, capacity)

    grad_gate_up = gate_up_sum.last()
    home_a = lax.ppermute(
        lax.dynamic_slice(grad_gate_up, (depth * c, 0), (depth, hidden_units)),
        ("yl", "c"),
        back(PAIR_A),
    ).astype(f32)
    home_b = lax.ppermute(
        lax.dynamic_slice(grad_gate_up, (depth * (1 - c), 0), (depth, hidden_units)),
        ("yl", "c"),
        back(PAIR_B),
    ).astype(f32)
    grad_down = lax.ppermute(grad_down, CYCLE_AXES, back(CYCLE)).astype(f32)
    even = jnp.where(yl == 0, home_a, home_b)
    odd = jnp.where(yl == 0, home_b, home_a)

    def natural(start):
        return jnp.concatenate(
            [
                v[:, start + k * quarter : start + (k + 1) * quarter]
                for k in range(2)
                for v in (even, odd)
            ],
            axis=1,
        )[None]

    new_gate_weight, new_gate_moment, new_gate_second = adamw(
        gate_weight, gate_moment, gate_second, natural(0)
    )
    new_up_weight, new_up_moment, new_up_second = adamw(
        up_weight, up_moment, up_second, natural(half)
    )
    new_down_weight, new_down_moment, new_down_second = adamw(
        down_weight, down_moment, down_second, grad_down[None]
    )
    return (
        input_grad,
        prob_grad.T,
        new_gate_weight,
        new_up_weight,
        new_down_weight,
        new_gate_moment,
        new_up_moment,
        new_down_moment,
        new_gate_second,
        new_up_second,
        new_down_second,
    )


def solution(mesh):
    fine = Mesh(mesh.devices.reshape(4, 2, 2, 4, 2), ("x", "yh", "yl", "z", "c"))
    tokens = P(("x", "yh", "yl", "z", "c"), None)
    weights = P(("z", "c"), ("x", "yh", "yl"), None)
    return jax.shard_map(
        body,
        mesh=fine,
        in_specs=(tokens,) * 4 + (weights,) * 9,
        out_specs=(tokens,) * 2 + (weights,) * 9,
        check_vma=False,
    )
```

time: 499 us -> 404 us (0.81)
  the two profiles are of different devices: /device:TPU:1 before, /device:TPU:8 now
where the time goes in v3:
time: 404 us; the launch traced here: 396 us
  waiting for transfers between devices  228 us (56%)
  starting transfers between devices  59.1 us (15%)
  matrix products  40 us (10%)
  local copies, waits for them, and re-layouts  34.8 us (9%)
  other arithmetic  28 us (7%)
  Pallas kernels  4.41 us (1%)
    ppermute x1, waiting for transfers between devices, body(): lax.ppermute(jnp.where(yl == 0, chunks[1], chunks[0]), ('yl', 'c'), PAIR_B)  53.9 us
    ppermute x3, waiting for transfers between devices, far(): lax.ppermute(left[:half], 'x', PLUS)  52.4 us
    ppermute x2, waiting for transfers between devices, second(): lax.ppermute(to_right, 'x', PLUS)  34.7 us
    ppermute x1, waiting for transfers between devices, body(): down_other = lax.ppermute(down_part, 'yh', SWAP)  25.8 us
    ppermute x1, waiting for transfers between devices, body(): grad_down = lax.ppermute(grad_down, CYCLE_AXES, back(CYCLE)).astype(f32)  20 us
    ppermute x4, waiting for transfers between devices, first(): self.got = (lax.ppermute(top, 'x', PLUS), lax.ppermute(low, 'x', MINUS))  16.3 us
    dot_general x2, matrix products, input_part(): lax.dot_general(d_rows, w_gate_up, (((1,), (1,)), ((), ())), preferred_el...  15 us
    dynamic_update_slice x14, local copies, waits for them, and re-layouts, put(): return lax.dynamic_update_slice(whole, part, (row, 0))  13.6 us
  transfers between devices with their start and end apart: 35, of which 15 were waited for; matrix products, arithmetic and copies ran while one was open for 19% of the time, Pallas kernels for 1%

profile of v3, /device:TPU:8, one launch (start us, length us, event | category | flops | bytes accessed | tf_op | source)
XLA Modules:
  0.0 396.2 jit_solution(14937928457777846399)
XLA Ops:
  4.2 2.1 pack_rows.1
  8.1 6.9 %all-to-all-start = ((bf16[8,48,5248]{2,1,0:T(8,128)(2,1)}), bf16[8,48,5248]{2,1,0:T(8,128)(2,1)}, u32[]{:S(2)}, u32[]{:S(2)}) async-start(bf16[8,48,5248]{2,1,0:T(8,128)(2,1)} %bitcast.44), calls=%async_computation | async-start | bytes 8060928 | tf_op jit(solution)/shard_map/all_to_all | solution.py:262
  15.6 2.5 collective-permute-start.3
  20.1 53.9 %collective-permute-done.4 = bf16[160,1536]{1,0:T(8,128)(2,1)S(1)} collective-permute-done((bf16[160,1536]{1,0:T(8,128)(2,1)S(1)}, bf16[160,1536]{1,0:T(8,128)(2,1)S(1)}, u32[]{:S(2)}, u32[]{:S(2)}) %collective-permute-start.4) | collective-permute-done | bytes 491552 | tf_op jit(solution)/shard_map/ppermute | solution.py:254
  74.0 5.3 %collective-permute-done.3 = bf16[160,1536]{1,0:T(8,128)(2,1)} collective-permute-done((bf16[160,1536]{1,0:T(8,128)(2,1)S(1)}, bf16[160,1536]{1,0:T(8,128)(2,1)}, u32[]{:S(2)}, u32[]{:S(2)}) %collective-permute-start.3) | collective-permute-done | bytes 491552 | tf_op jit(solution)/shard_map/ppermute | solution.py:253
  79.3 3.6 broadcast_in_dim.7
  82.8 2.8 constant_dynamic-update-slice_fusion.9
  87.7 3.8 collective-permute-start.5
  91.6 25.8 %collective-permute-done.2 = bf16[96,2560]{1,0:T(8,128)(2,1)} collective-permute-done((bf16[96,2560]{1,0:T(8,128)(2,1)S(1)}, bf16[96,2560]{1,0:T(8,128)(2,1)}, u32[]{:S(2)}, u32[]{:S(2)}) %collective-permute-start.2) | collective-permute-done | bytes 491552 | tf_op jit(solution)/shard_map/ppermute | solution.py:267
  118.8 3.0 collective-permute-start.9
  122.6 3.2 collective-permute-start.11
  127.0 2.2 constant_dynamic-update-slice_fusion.8
  130.2 19.0 %collective-permute-done.10 = bf16[160,1536]{1,0:T(8,128)(2,1)S(1)} collective-permute-done((bf16[160,1536]{1,0:T(8,128)(2,1)S(1)}, bf16[160,1536]{1,0:T(8,128)(2,1)S(1)}, u32[]{:S(2)}, u32[]{:S(2)}) %collective-permute-start.10) | collective-permute-done | bytes 491552 | tf_op jit(solution)/shard_map/ppermute | solution.py:167
  150.9 2.2 constant_dynamic-update-slice_fusion.4
  159.8 2.2 constant_dynamic-update-slice_fusion.3
  162.1 2.2 constant_dynamic-update-slice_fusion.2
  164.3 24.8 %collective-permute-done.16 = bf16[160,1536]{1,0:T(8,128)(2,1)S(1)} collective-permute-done((bf16[160,1536]{1,0:T(8,128)(2,1)S(1)}, bf16[160,1536]{1,0:T(8,128)(2,1)S(1)}, u32[]{:S(2)}, u32[]{:S(2)}) %collective-permute-start.16) | collective-permute-done | bytes 491552 | tf_op jit(solution)/shard_map/ppermute | solution.py:167
  190.9 2.2 collective-permute-start.14
  193.4 2.4 fusion.22
  196.7 8.6 %collective-permute-done.14 = bf16[96,2560]{1,0:T(8,128)(2,1)S(1)} collective-permute-done((bf16[96,2560]{1,0:T(8,128)(2,1)S(1)}, bf16[96,2560]{1,0:T(8,128)(2,1)S(1)}, u32[]{:S(2)}, u32[]{:S(2)}) %collective-permute-start.14) | collective-permute-done | bytes 491552 | tf_op jit(solution)/shard_map/ppermute | solution.py:167
  205.8 9.3 %fusion.1 = f32[768,1536]{0,1:T(8,128)S(1)} fusion(bf16[2560,1536]{1,0:T(8,128)(2,1)} %constant_dynamic-update-slice_fusion, bf16[384,2560]{1,0:T(8,128)(2,1)S(1)} %get-tuple-element.61, bf16[384,2560]{1,0:T(8,128)(2,1)S(1)} %get-tuple-element.59), kind=kOutput, calls=%fused_computation.7 | convolution fusion | flops 6047662080 | bytes 16515072 | tf_op jit(solution)/shard_map/dot_general | solution.py:296
  215.0 3.3 convolution_convert_fusion.1
  219.1 2.7 collective-permute-start.21
  221.8 4.2 %multiply_convert_fusion.2 = (bf16[768,768]{0,1:T(8,128)(2,1)S(1)}, bf16[768,768]{0,1:T(8,128)(2,1)S(1)}, f32[768]{0:T(1024)S(1)}) fusion(f32[768,1536]{0,1:T(8,128)S(1)} %fusion.1, f32[768]{0:T(1024)S(1)} %convert_reduce_fusion, bf16[768,2560]{1,0:T(8,128)(2,1)S(1)} %constant_dynamic-update-slice_fusion.10, bf16[384,2560]{1,0:T(8,128)(2,1)S(1)} %get-tuple-element.62, ...), kind=kOutput, calls=%fused_computation.13 | convolution fusion | flops 3038969088 | bytes 14948352 | tf_op jit(solution)/shard_map/dot_general | solution.py:309
  226.0 5.8 %collective-permute-done.20 = bf16[96,2560]{1,0:T(8,128)(2,1)S(1)} collective-permute-done((bf16[96,2560]{1,0:T(8,128)(2,1)S(1)}, bf16[96,2560]{1,0:T(8,128)(2,1)S(1)}, u32[]{:S(2)}, u32[]{:S(2)}) %collective-permute-start.20) | collective-permute-done | bytes 491552 | tf_op jit(solution)/shard_map/ppermute | solution.py:196
  232.3 3.4 collective-permute-start.23
  235.7 8.3 %convolution_convert_fusion = bf16[2560,1536]{1,0:T(8,128)(2,1)S(1)} fusion(bf16[384,2560]{1,0:T(8,128)(2,1)S(1)} %get-tuple-element.61, bf16[384,2560]{1,0:T(8,128)(2,1)S(1)} %get-tuple-element.59, bf16[768,768]{0,1:T(8,128)(2,1)S(1)} %get-tuple-element.57, bf16[768,768]{0,1:T(8,128)(2,1)S(1)} %get-tuple-element.56), kind=kOutput, calls=%fused_computation | convolution fusion | flops 6056312832 | bytes 14155776 | tf_op jit(solution)/shard_map/dot_general | solution.py:318
  244.3 10.8 %collective-permute-done.22 = bf16[192,2560]{1,0:T(8,128)(2,1)S(1)} collective-permute-done((bf16[192,2560]{1,0:T(8,128)(2,1)S(1)}, bf16[192,2560]{1,0:T(8,128)(2,1)S(1)}, u32[]{:S(2)}, u32[]{:S(2)}) %collective-permute-start.22) | collective-permute-done | bytes 983072 | tf_op jit(solution)/shard_map/ppermute | solution.py:204
  256.1 2.3 collective-permute-start.25
  258.5 7.9 %convolution_convert_fusion.2 = bf16[384,2560]{1,0:T(8,128)(2,1)} fusion(bf16[2560,1536]{1,0:T(8,128)(2,1)} %constant_dynamic-update-slice_fusion, bf16[768,1536]{0,1:T(8,128)(2,1)S(1)} %pad_maximum_fusion.6), kind=kOutput, calls=%fused_computation.3 | convolution fusion | flops 3020881920 | bytes 11010048 | tf_op jit(solution)/shard_map/dot_general | solution.py:328
  266.4 10.5 %collective-permute-done.24 = bf16[320,1536]{1,0:T(8,128)(2,1)S(1)} collective-permute-done((bf16[320,1536]{1,0:T(8,128)(2,1)S(1)}, bf16[320,1536]{1,0:T(8,128)(2,1)S(1)}, u32[]{:S(2)}, u32[]{:S(2)}) %collective-permute-start.24) | collective-permute-done | bytes 983072 | tf_op jit(solution)/shard_map/ppermute | solution.py:196
  281.4 2.3 collective-permute-start.27
  286.2 2.3 add_convert_fusion.6
  288.5 3.2 collective-permute-start.31
  291.7 7.1 %fusion = bf16[384,2560]{1,0:T(8,128)(2,1)S(1)} fusion(bf16[2560,1536]{1,0:T(8,128)(2,1)} %constant_dynamic-update-slice_fusion, bf16[384,2560]{1,0:T(8,128)(2,1)} %collective-permute-done.18, bf16[768,1536]{0,1:T(8,128)(2,1)S(1)} %pad_maximum_fusion.6), kind=kOutput, calls=%fused_computation.4 | convolution fusion | flops 3022848000 | bytes 12976128 | tf_op jit(solution)/shard_map/dot_general | solution.py:328
  298.8 24.0 %collective-permute-done.26 = bf16[640,1536]{1,0:T(8,128)(2,1)} collective-permute-done((bf16[640,1536]{1,0:T(8,128)(2,1)}, bf16[640,1536]{1,0:T(8,128)(2,1)}, u32[]{:S(2)}, u32[]{:S(2)}) %collective-permute-start.26) | collective-permute-done | bytes 1966112 | tf_op jit(solution)/shard_map/ppermute | solution.py:204
  322.7 3.1 add_convert_fusion.1
  325.8 3.0 collective-permute-start.28
  330.3 5.4 %all-to-all-start.1 = ((bf16[8,48,2688]{2,1,0:T(8,128)(2,1)}), bf16[8,48,2688]{2,1,0:T(8,128)(2,1)S(1)}, u32[]{:S(2)}, u32[]{:S(2)}) async-start(bf16[8,48,2688]{2,1,0:T(8,128)(2,1)} %bitcast.48), calls=%async_computation.1 | async-start | bytes 4128768 | tf_op jit(solution)/shard_map/all_to_all | solution.py:339
  339.5 12.9 %collective-permute-done.28 = bf16[320,1536]{1,0:T(8,128)(2,1)} collective-permute-done((bf16[320,1536]{1,0:T(8,128)(2,1)}, bf16[320,1536]{1,0:T(8,128)(2,1)}, u32[]{:S(2)}, u32[]{:S(2)}) %collective-permute-start.28) | collective-permute-done | bytes 983072 | tf_op jit(solution)/shard_map/ppermute | solution.py:212
  352.3 2.6 add_convert_fusion
  357.9 20.0 %collective-permute-done.32 = bf16[96,2560]{1,0:T(8,128)(2,1)S(1)} collective-permute-done((bf16[96,2560]{1,0:T(8,128)(2,1)S(1)}, bf16[96,2560]{1,0:T(8,128)(2,1)S(1)}, u32[]{:S(2)}, u32[]{:S(2)}) %collective-permute-start.32) | collective-permute-done | bytes 491552 | tf_op jit(solution)/shard_map/ppermute | solution.py:355
  378.0 2.1 multiply_subtract_fusion
  380.1 2.4 all-to-all-done.1
  382.4 2.3 unpack_rows.1
  384.8 3.0 collective-permute-done.30
  390.9 2.1 multiply_subtract_fusion.1
  393.7 2.1 multiply_subtract_fusion.2
  (129 shorter events, 47.8 us)
Async XLA Ops:
  8.1 6.9 %copy-start.10 = (f32[1,160,1536]{2,1,0:T(8,128)S(1)}, f32[1,160,1536]{2,1,0:T(8,128)}, u32[]{:S(2)}) copy-start(f32[1,160,1536]{2,1,0:T(8,128)} %param.17) | copy-start | bytes 2949124
  8.1 7.0 %copy-start.8 = (f32[1,160,1536]{2,1,0:T(8,128)S(1)}, f32[1,160,1536]{2,1,0:T(8,128)}, u32[]{:S(2)}) copy-start(f32[1,160,1536]{2,1,0:T(8,128)} %param.18) | copy-start | bytes 2949124
  8.1 141.9 %all-to-all-start = ((bf16[8,48,5248]{2,1,0:T(8,128)(2,1)}), bf16[8,48,5248]{2,1,0:T(8,128)(2,1)}, u32[]{:S(2)}, u32[]{:S(2)}) async-start(bf16[8,48,5248]{2,1,0:T(8,128)(2,1)} %bitcast.44), calls=%async_computation | async-start | bytes 8060928 | tf_op jit(solution)/shard_map/all_to_all | solution.py:262
  15.1 3.0 copy-start.6
  15.5 58.5 %collective-permute-start.4 = (bf16[160,1536]{1,0:T(8,128)(2,1)S(1)}, bf16[160,1536]{1,0:T(8,128)(2,1)S(1)}, u32[]{:S(2)}, u32[]{:S(2)}) collective-permute-start(bf16[160,1536]{1,0:T(8,128)(2,1)S(1)} %get-tuple-element.81), channel_id=1, source_target_pairs={{0,1},{1,9},{8,0},{9,8},{2,3},{3,11},{10,2},{11,10},{4,5},{5,13},{... | collective-permute-start | bytes 1474568 | tf_op jit(solution)/shard_map/ppermute | solution.py:254
  15.6 63.7 %collective-permute-start.3 = (bf16[160,1536]{1,0:T(8,128)(2,1)S(1)}, bf16[160,1536]{1,0:T(8,128)(2,1)}, u32[]{:S(2)}, u32[]{:S(2)}) collective-permute-start(bf16[160,1536]{1,0:T(8,128)(2,1)S(1)} %get-tuple-element.82), channel_id=1, source_target_pairs={{0,0},{1,8},{8,1},{9,9},{2,2},{3,10},{10,3},{11,11},{4,4},{5,12},{... | collective-permute-start | bytes 1474568 | tf_op jit(solution)/shard_map/ppermute | solution.py:253
  18.2 73.4 %collective-permute-start.1 = (bf16[96,2560]{1,0:T(8,128)(2,1)S(1)}, bf16[96,2560]{1,0:T(8,128)(2,1)S(1)}, u32[]{:S(2)}, u32[]{:S(2)}) collective-permute-start(bf16[96,2560]{1,0:T(8,128)(2,1)S(1)} %convert_bitcast_fusion.2), channel_id=1, source_target_pairs={{0,0},{1,8},{8,16},{9,24},{16,32},{17,40},{24,48},{25,56},{32,1},{... | collective-permute-start | bytes 1474568 | tf_op jit(solution)/shard_map/ppermute | solution.py:258
  85.6 33.1 %collective-permute-start.7 = (bf16[320,1536]{1,0:T(8,128)(2,1)}, bf16[320,1536]{1,0:T(8,128)(2,1)S(1)}, u32[]{:S(2)}, u32[]{:S(2)}) collective-permute-start(bf16[320,1536]{1,0:T(8,128)(2,1)} %get-tuple-element.49), channel_id=1, source_target_pairs={{0,96},{32,0},{64,32},{96,64},{1,97},{33,1},{65,33},{97,65},{2,98}... | collective-permute-start | bytes 2949128 | tf_op jit(solution)/shard_map/ppermute | solution.py:163
  85.6 33.1 %collective-permute-start.6 = (bf16[320,1536]{1,0:T(8,128)(2,1)}, bf16[320,1536]{1,0:T(8,128)(2,1)}, u32[]{:S(2)}, u32[]{:S(2)}) collective-permute-start(bf16[320,1536]{1,0:T(8,128)(2,1)} %get-tuple-element.49), channel_id=1, source_target_pairs={{0,32},{32,64},{64,96},{96,0},{1,33},{33,65},{65,97},{97,1},{2,34}... | collective-permute-start | bytes 2949128 | tf_op jit(solution)/shard_map/ppermute | solution.py:163
  87.7 31.1 %collective-permute-start.5 = (bf16[320,1536]{1,0:T(8,128)(2,1)}, bf16[320,1536]{1,0:T(8,128)(2,1)}, u32[]{:S(2)}, u32[]{:S(2)}) collective-permute-start(bf16[320,1536]{1,0:T(8,128)(2,1)} %get-tuple-element.49), channel_id=1, source_target_pairs={{0,16},{16,0},{1,17},{17,1},{2,18},{18,2},{3,19},{19,3},{4,20},{20... | collective-permute-start | bytes 2949128 | tf_op jit(solution)/shard_map/ppermute | solution.py:266
  91.5 25.8 %collective-permute-start.2 = (bf16[96,2560]{1,0:T(8,128)(2,1)S(1)}, bf16[96,2560]{1,0:T(8,128)(2,1)}, u32[]{:S(2)}, u32[]{:S(2)}) collective-permute-start(bf16[96,2560]{1,0:T(8,128)(2,1)S(1)} %collective-permute-done.1), channel_id=1, source_target_pairs={{0,16},{16,0},{1,17},{17,1},{2,18},{18,2},{3,19},{19,3},{4,20},{20... | collective-permute-start | bytes 1474568 | tf_op jit(solution)/shard_map/ppermute | solution.py:267
  118.8 34.4 %collective-permute-start.9 = (bf16[320,1536]{1,0:T(8,128)(2,1)}, bf16[320,1536]{1,0:T(8,128)(2,1)}, u32[]{:S(2)}, u32[]{:S(2)}) collective-permute-start(bf16[320,1536]{1,0:T(8,128)(2,1)} %collective-permute-done.5), channel_id=1, source_target_pairs={{0,96},{32,0},{64,32},{96,64},{1,97},{33,1},{65,33},{97,65},{2,98}... | collective-permute-start | bytes 2949128 | tf_op jit(solution)/shard_map/ppermute | solution.py:163
  121.8 31.4 %collective-permute-start.8 = (bf16[320,1536]{1,0:T(8,128)(2,1)}, bf16[320,1536]{1,0:T(8,128)(2,1)}, u32[]{:S(2)}, u32[]{:S(2)}) collective-permute-start(bf16[320,1536]{1,0:T(8,128)(2,1)} %collective-permute-done.5), channel_id=1, source_target_pairs={{0,32},{32,64},{64,96},{96,0},{1,33},{33,65},{65,97},{97,1},{2,34}... | collective-permute-start | bytes 2949128 | tf_op jit(solution)/shard_map/ppermute | solution.py:163
  122.6 27.5 %collective-permute-start.11 = (bf16[160,1536]{1,0:T(8,128)(2,1)}, bf16[160,1536]{1,0:T(8,128)(2,1)S(1)}, u32[]{:S(2)}, u32[]{:S(2)}) collective-permute-start(bf16[160,1536]{1,0:T(8,128)(2,1)} %slice.155), channel_id=1, source_target_pairs={{0,96},{32,0},{64,32},{96,64},{1,97},{33,1},{65,33},{97,65},{2,98}... | collective-permute-start | bytes 1474568 | tf_op jit(solution)/shard_map/ppermute | solution.py:167
  126.9 22.3 %collective-permute-start.10 = (bf16[160,1536]{1,0:T(8,128)(2,1)S(1)}, bf16[160,1536]{1,0:T(8,128)(2,1)S(1)}, u32[]{:S(2)}, u32[]{:S(2)}) collective-permute-start(bf16[160,1536]{1,0:T(8,128)(2,1)S(1)} %slice.154), channel_id=1, source_target_pairs={{0,32},{32,64},{64,96},{96,0},{1,33},{33,65},{65,97},{97,1},{2,34}... | collective-permute-start | bytes 1474568 | tf_op jit(solution)/shard_map/ppermute | solution.py:167
  150.0 55.3 %collective-permute-start = (bf16[384,5248]{1,0:T(8,128)(2,1)}, bf16[384,5248]{1,0:T(8,128)(2,1)S(1)}, u32[]{:S(2)}, u32[]{:S(2)}) collective-permute-start(bf16[384,5248]{1,0:T(8,128)(2,1)} %bitcast.3), channel_id=1, source_target_pairs={{0,1},{1,0},{2,3},{3,2},{4,5},{5,4},{6,7},{7,6},{8,9},{9,8},{10,11... | collective-permute-start | bytes 12091400 | tf_op jit(solution)/shard_map/ppermute | solution.py:291
  153.1 37.6 %collective-permute-start.13 = (bf16[192,2560]{1,0:T(8,128)(2,1)S(1)}, bf16[192,2560]{1,0:T(8,128)(2,1)S(1)}, u32[]{:S(2)}, u32[]{:S(2)}) collective-permute-start(bf16[192,2560]{1,0:T(8,128)(2,1)S(1)} %maximum_select_fusion), channel_id=1, source_target_pairs={{0,96},{32,0},{64,32},{96,64},{1,97},{33,1},{65,33},{97,65},{2,98}... | collective-permute-start | bytes 2949128 | tf_op jit(solution)/shard_map/ppermute | solution.py:163
  153.1 37.7 %collective-permute-start.12 = (bf16[192,2560]{1,0:T(8,128)(2,1)S(1)}, bf16[192,2560]{1,0:T(8,128)(2,1)S(1)}, u32[]{:S(2)}, u32[]{:S(2)}) collective-permute-start(bf16[192,2560]{1,0:T(8,128)(2,1)S(1)} %maximum_select_fusion), channel_id=1, source_target_pairs={{0,32},{32,64},{64,96},{96,0},{1,33},{33,65},{65,97},{97,1},{2,34}... | collective-permute-start | bytes 2949128 | tf_op jit(solution)/shard_map/ppermute | solution.py:163
  156.2 33.7 %collective-permute-start.17 = (bf16[160,1536]{1,0:T(8,128)(2,1)S(1)}, bf16[160,1536]{1,0:T(8,128)(2,1)S(1)}, u32[]{:S(2)}, u32[]{:S(2)}) collective-permute-start(bf16[160,1536]{1,0:T(8,128)(2,1)S(1)} %slice.161), channel_id=1, source_target_pairs={{0,96},{32,0},{64,32},{96,64},{1,97},{33,1},{65,33},{97,65},{2,98}... | collective-permute-start | bytes 1474568 | tf_op jit(solution)/shard_map/ppermute | solution.py:167
  158.7 30.5 %collective-permute-start.16 = (bf16[160,1536]{1,0:T(8,128)(2,1)S(1)}, bf16[160,1536]{1,0:T(8,128)(2,1)S(1)}, u32[]{:S(2)}, u32[]{:S(2)}) collective-permute-start(bf16[160,1536]{1,0:T(8,128)(2,1)S(1)} %slice.160), channel_id=1, source_target_pairs={{0,32},{32,64},{64,96},{96,0},{1,33},{33,65},{65,97},{97,1},{2,34}... | collective-permute-start | bytes 1474568 | tf_op jit(solution)/shard_map/ppermute | solution.py:167
  190.8 14.5 %collective-permute-start.15 = (bf16[96,2560]{1,0:T(8,128)(2,1)S(1)}, bf16[96,2560]{1,0:T(8,128)(2,1)S(1)}, u32[]{:S(2)}, u32[]{:S(2)}) collective-permute-start(bf16[96,2560]{1,0:T(8,128)(2,1)S(1)} %slice.157), channel_id=1, source_target_pairs={{0,96},{32,0},{64,32},{96,64},{1,97},{33,1},{65,33},{97,65},{2,98}... | collective-permute-start | bytes 1474568 | tf_op jit(solution)/shard_map/ppermute | solution.py:167
  190.9 14.3 %collective-permute-start.14 = (bf16[96,2560]{1,0:T(8,128)(2,1)S(1)}, bf16[96,2560]{1,0:T(8,128)(2,1)S(1)}, u32[]{:S(2)}, u32[]{:S(2)}) collective-permute-start(bf16[96,2560]{1,0:T(8,128)(2,1)S(1)} %slice.156), channel_id=1, source_target_pairs={{0,32},{32,64},{64,96},{96,0},{1,33},{33,65},{65,97},{97,1},{2,34}... | collective-permute-start | bytes 1474568 | tf_op jit(solution)/shard_map/ppermute | solution.py:167
  218.4 13.4 %copy-start.7 = (bf16[768,2560]{1,0:T(8,128)(2,1)}, bf16[768,2560]{1,0:T(8,128)(2,1)S(1)}, u32[]{:S(2)}) copy-start(bf16[768,2560]{1,0:T(8,128)(2,1)S(1)} %convolution_convert_fusion.1) | copy-start | bytes 11796484
  218.5 13.2 %collective-permute-start.20 = (bf16[96,2560]{1,0:T(8,128)(2,1)S(1)}, bf16[96,2560]{1,0:T(8,128)(2,1)S(1)}, u32[]{:S(2)}, u32[]{:S(2)}) collective-permute-start(bf16[96,2560]{1,0:T(8,128)(2,1)S(1)} %get-tuple-element.30), channel_id=1, source_target_pairs={{0,32},{32,64},{64,96},{96,0},{1,33},{33,65},{65,97},{97,1},{2,34}... | collective-permute-start | bytes 1474568 | tf_op jit(solution)/shard_map/ppermute | solution.py:196
  219.1 12.7 %collective-permute-start.21 = (bf16[96,2560]{1,0:T(8,128)(2,1)S(1)}, bf16[96,2560]{1,0:T(8,128)(2,1)S(1)}, u32[]{:S(2)}, u32[]{:S(2)}) collective-permute-start(bf16[96,2560]{1,0:T(8,128)(2,1)S(1)} %get-tuple-element.31), channel_id=1, source_target_pairs={{0,96},{32,0},{64,32},{96,64},{1,97},{33,1},{65,33},{97,65},{2,98}... | collective-permute-start | bytes 1474568 | tf_op jit(solution)/shard_map/ppermute | solution.py:196
  232.2 22.8 %collective-permute-start.22 = (bf16[192,2560]{1,0:T(8,128)(2,1)S(1)}, bf16[192,2560]{1,0:T(8,128)(2,1)S(1)}, u32[]{:S(2)}, u32[]{:S(2)}) collective-permute-start(bf16[192,2560]{1,0:T(8,128)(2,1)S(1)} %pad_maximum_fusion.10), channel_id=1, source_target_pairs={{0,32},{32,64},{64,96},{96,0},{1,33},{33,65},{65,97},{97,1},{2,34}... | collective-permute-start | bytes 2949128 | tf_op jit(solution)/shard_map/ppermute | solution.py:204
  232.3 22.8 %collective-permute-start.23 = (bf16[192,2560]{1,0:T(8,128)(2,1)S(1)}, bf16[192,2560]{1,0:T(8,128)(2,1)S(1)}, u32[]{:S(2)}, u32[]{:S(2)}) collective-permute-start(bf16[192,2560]{1,0:T(8,128)(2,1)S(1)} %pad_maximum_fusion.11), channel_id=1, source_target_pairs={{0,96},{32,0},{64,32},{96,64},{1,97},{33,1},{65,33},{97,65},{2,98}... | collective-permute-start | bytes 2949128 | tf_op jit(solution)/shard_map/ppermute | solution.py:204
  244.0 33.0 %copy-start.5 = (bf16[2560,1536]{1,0:T(8,128)(2,1)}, bf16[2560,1536]{1,0:T(8,128)(2,1)S(1)}, u32[]{:S(2)}) copy-start(bf16[2560,1536]{1,0:T(8,128)(2,1)S(1)} %convolution_convert_fusion) | copy-start | bytes 23592964
  255.0 3.5 copy-start.18
  255.0 3.5 copy-start.19
  255.0 21.9 %collective-permute-start.24 = (bf16[320,1536]{1,0:T(8,128)(2,1)S(1)}, bf16[320,1536]{1,0:T(8,128)(2,1)S(1)}, u32[]{:S(2)}, u32[]{:S(2)}) collective-permute-start(bf16[320,1536]{1,0:T(8,128)(2,1)S(1)} %get-tuple-element.34), channel_id=1, source_target_pairs={{0,32},{32,64},{64,96},{96,0},{1,33},{33,65},{65,97},{97,1},{2,34}... | collective-permute-start | bytes 2949128 | tf_op jit(solution)/shard_map/ppermute | solution.py:196
  256.1 20.9 %collective-permute-start.25 = (bf16[320,1536]{1,0:T(8,128)(2,1)S(1)}, bf16[320,1536]{1,0:T(8,128)(2,1)S(1)}, u32[]{:S(2)}, u32[]{:S(2)}) collective-permute-start(bf16[320,1536]{1,0:T(8,128)(2,1)S(1)} %get-tuple-element.35), channel_id=1, source_target_pairs={{0,96},{32,0},{64,32},{96,64},{1,97},{33,1},{65,33},{97,65},{2,98}... | collective-permute-start | bytes 2949128 | tf_op jit(solution)/shard_map/ppermute | solution.py:196
  266.4 25.3 %collective-permute-start.18 = (bf16[384,2560]{1,0:T(8,128)(2,1)}, bf16[384,2560]{1,0:T(8,128)(2,1)}, u32[]{:S(2)}, u32[]{:S(2)}) collective-permute-start(bf16[384,2560]{1,0:T(8,128)(2,1)} %convolution_convert_fusion.2), channel_id=1, source_target_pairs={{0,1},{1,0},{2,3},{3,2},{4,5},{5,4},{6,7},{7,6},{8,9},{9,8},{10,11... | collective-permute-start | bytes 5898248 | tf_op jit(solution)/shard_map/ppermute | solution.py:332
  280.4 42.3 %collective-permute-start.26 = (bf16[640,1536]{1,0:T(8,128)(2,1)}, bf16[640,1536]{1,0:T(8,128)(2,1)}, u32[]{:S(2)}, u32[]{:S(2)}) collective-permute-start(bf16[640,1536]{1,0:T(8,128)(2,1)} %pad_maximum_fusion.8), channel_id=1, source_target_pairs={{0,32},{32,64},{64,96},{96,0},{1,33},{33,65},{65,97},{97,1},{2,34}... | collective-permute-start | bytes 5898248 | tf_op jit(solution)/shard_map/ppermute | solution.py:204
  281.4 41.3 %collective-permute-start.27 = (bf16[640,1536]{1,0:T(8,128)(2,1)}, bf16[640,1536]{1,0:T(8,128)(2,1)}, u32[]{:S(2)}, u32[]{:S(2)}) collective-permute-start(bf16[640,1536]{1,0:T(8,128)(2,1)} %pad_maximum_fusion.9), channel_id=1, source_target_pairs={{0,96},{32,0},{64,32},{96,64},{1,97},{33,1},{65,33},{97,65},{2,98}... | collective-permute-start | bytes 5898248 | tf_op jit(solution)/shard_map/ppermute | solution.py:204
  284.4 1.7 collective-permute-start.19
  288.5 47.2 %collective-permute-start.31 = (bf16[96,2560]{1,0:T(8,128)(2,1)}, bf16[96,2560]{1,0:T(8,128)(2,1)}, u32[]{:S(2)}, u32[]{:S(2)}) collective-permute-start(bf16[96,2560]{1,0:T(8,128)(2,1)} %add_convert_fusion.6), channel_id=1, source_target_pairs={{0,16},{16,0},{1,17},{17,1},{2,18},{18,2},{3,19},{19,3},{4,20},{20... | collective-permute-start | bytes 1474568 | tf_op jit(solution)/shard_map/ppermute | solution.py:212
  325.8 26.5 %collective-permute-start.28 = (bf16[320,1536]{1,0:T(8,128)(2,1)}, bf16[320,1536]{1,0:T(8,128)(2,1)}, u32[]{:S(2)}, u32[]{:S(2)}) collective-permute-start(bf16[320,1536]{1,0:T(8,128)(2,1)} %add_convert_fusion.1), channel_id=1, source_target_pairs={{0,16},{16,0},{1,17},{17,1},{2,18},{18,2},{3,19},{19,3},{4,20},{20... | collective-permute-start | bytes 2949128 | tf_op jit(solution)/shard_map/ppermute | solution.py:212
  330.3 52.1 %all-to-all-start.1 = ((bf16[8,48,2688]{2,1,0:T(8,128)(2,1)}), bf16[8,48,2688]{2,1,0:T(8,128)(2,1)S(1)}, u32[]{:S(2)}, u32[]{:S(2)}) async-start(bf16[8,48,2688]{2,1,0:T(8,128)(2,1)} %bitcast.48), calls=%async_computation.1 | async-start | bytes 4128768 | tf_op jit(solution)/shard_map/all_to_all | solution.py:339
  337.4 40.6 %copy-start.12 = (f32[1,96,2560]{2,1,0:T(8,128)S(1)}, f32[1,96,2560]{2,1,0:T(8,128)}, u32[]{:S(2)}) copy-start(f32[1,96,2560]{2,1,0:T(8,128)} %param.22) | copy-start | bytes 2949124
  337.4 40.6 %copy-start.13 = (f32[1,96,2560]{2,1,0:T(8,128)S(1)}, f32[1,96,2560]{2,1,0:T(8,128)}, u32[]{:S(2)}) copy-start(f32[1,96,2560]{2,1,0:T(8,128)} %param.25) | copy-start | bytes 2949124
  337.4 40.6 %collective-permute-start.32 = (bf16[96,2560]{1,0:T(8,128)(2,1)S(1)}, bf16[96,2560]{1,0:T(8,128)(2,1)S(1)}, u32[]{:S(2)}, u32[]{:S(2)}) collective-permute-start(bf16[96,2560]{1,0:T(8,128)(2,1)S(1)} %add_convert_fusion.5), channel_id=1, source_target_pairs={{0,0},{8,1},{16,8},{24,9},{32,16},{40,17},{48,24},{56,25},{1,32},{... | collective-permute-start | bytes 1474568 | tf_op jit(solution)/shard_map/ppermute | solution.py:355
  355.9 28.9 %collective-permute-start.29 = (bf16[160,1536]{1,0:T(8,128)(2,1)}, bf16[160,1536]{1,0:T(8,128)(2,1)S(1)}, u32[]{:S(2)}, u32[]{:S(2)}) collective-permute-start(bf16[160,1536]{1,0:T(8,128)(2,1)} %get-tuple-element.79), channel_id=1, source_target_pairs={{0,0},{8,1},{1,8},{9,9},{2,2},{10,3},{3,10},{11,11},{4,4},{12,5},{... | collective-permute-start | bytes 1474568 | tf_op jit(solution)/shard_map/ppermute | solution.py:345
  357.8 24.6 %copy-start.4 = (s32[128,2]{0,1:T(2,128)S(1)}, s32[128,2]{0,1:T(2,128)}, u32[]{:S(2)}) copy-start(s32[128,2]{0,1:T(2,128)} %param.15) | copy-start | bytes 3076
  357.8 30.0 %collective-permute-start.30 = (bf16[160,1536]{1,0:T(8,128)(2,1)}, bf16[160,1536]{1,0:T(8,128)(2,1)}, u32[]{:S(2)}, u32[]{:S(2)}) collective-permute-start(bf16[160,1536]{1,0:T(8,128)(2,1)} %get-tuple-element.80), channel_id=1, source_target_pairs={{1,0},{9,1},{0,8},{8,9},{3,2},{11,3},{2,10},{10,11},{5,4},{13,5},{... | collective-permute-start | bytes 1474568 | tf_op jit(solution)/shard_map/ppermute | solution.py:350
  390.9 2.1 copy-start.11
  390.9 2.2 copy-start.16
  390.9 2.9 copy-start.17
  (7 other events, 9.2 us)
